TPU v7x, 128 devices: a whole 4x4x4 slice. The times are simulated.
128 devices in a mesh: ctx: 16 (over x, y), head: 8 (over z, core).
Axes of the slice: x: 4, y: 4, z: 4, core: 2. Of those that a mesh axis runs over, the one named last changes fastest.
Arguments:
- tokens: bfloat16 [8192, 5376], P('ctx'), may hold values from -16 to 16
- norm_gain: bfloat16 [5376], replicated, may hold values from 0.099609375 to 1.8984375
- w_query: bfloat16 [5376, 4096], P(None, 'head'), may hold values from -4 to 4
- w_key: bfloat16 [5376, 2048], P(None, 'head'), may hold values from -1 to 1
- value_weight: bfloat16 [5376, 2048], P(None, 'head'), may hold values from -0.078125 to 0.078125
- w_out: bfloat16 [4096, 5376], P('head'), may hold values from -0.09375 to 0.09375
- mask_logit: float32 [32], P('head'), may hold values from -2 to 2
- noise_draw: float32 [32], P('head'), may hold values from 0.02 to 0.98
- cotangent: bfloat16 [8192, 5376], P('ctx'), may hold values from -16 to 16
Outputs:
- layer_out: bfloat16 [8192, 5376], P('ctx', 'head')
- grad_logit: float32 [32], P('head')
- grad_out_proj: float32 [4096, 5376], P('head', 'ctx')
All inputs are finite; a program needn't handle non-finite values.
Results may differ from a plain program's by a relative error of at most 0.025.
Values may be sent and summed in bfloat16 or wider, within the bound.
A program may use at most 128 MiB of HBM per device.

v0:
```python
import math

import jax
import jax.numpy as jnp
from jax import lax
from jax.sharding import PartitionSpec as P

HEAD_SIZE = 128
WINDOW_TOKENS = 1024


EPSILON = 1e-06
BETA = 2.0 / 3.0
GAMMA = -0.1
ZETA = 1.1
PENALTY = 0.1
SCORE_SCALE = 168.0 ** (-0.5)
TRANSPOSED = (((0,), (0,)), ((), ()))


def shifted_2(value, axis, steps):
    count = lax.axis_size(axis)
    first, last = (max(0, -steps), min(count, count - steps))
    return lax.ppermute(value, axis, [(source, source + steps) for source in range(first, last)])


def cut_along(value, dim, length):
    before, after = (value.shape[:dim], value.shape[dim + 1 :])
    return jnp.moveaxis(value.reshape(*before, length, -1, *after), dim, 0)


def sum_at_owner(value, axis, dim):
    length = lax.axis_size(axis)
    parts = lax.all_to_all(cut_along(value, dim, length), axis, 0, 0, tiled=True)
    return jnp.sum(parts.astype(jnp.float32), axis=0)


def copy_for_each(value, axis):
    copies = jnp.broadcast_to(value, (lax.axis_size(axis), *value.shape))
    return lax.all_to_all(copies, axis, split_axis=0, concat_axis=0, tiled=True)


def of_everyone(value, axis):
    return copy_for_each(value, axis).sum(axis=0)


def hard_concrete(mask_logit, noise_draw):
    stretched = jax.nn.sigmoid(
        (jnp.log(noise_draw) - jnp.log(1.0 - noise_draw) + mask_logit) / BETA
    )
    shifted = stretched * (ZETA - GAMMA) + GAMMA
    gate_value = jnp.clip(shifted, 0.0, 1.0)
    inside = jnp.logical_and(shifted > 0.0, shifted < 1.0)
    gate_slope = jnp.where(inside, (ZETA - GAMMA) * stretched * (1.0 - stretched) / BETA, 0.0)
    expected = jax.nn.sigmoid(mask_logit - BETA * math.log(-GAMMA / ZETA))
    return (gate_value, gate_slope, PENALTY * expected * (1.0 - expected))


def body(tokens, norm_gain, w_query, w_key, value_weight, w_out, mask_logit, noise_draw, cotangent):
    tok_rows = tokens.shape[0]
    local_heads = mask_logit.shape[0]
    local_kv = w_key.shape[1] // HEAD_SIZE
    group_count_heads = local_heads // local_kv
    context = lax.axis_size("ctx")
    position = lax.axis_index("ctx")
    inv_root = 1.0 / math.sqrt(tok_rows * context)
    widened = tokens.astype(jnp.float32)
    moment = jnp.mean(jnp.square(widened), axis=1, keepdims=True)
    normed = (
        widened * lax.rsqrt(moment + EPSILON) * norm_gain.astype(jnp.float32)[None, :]
    ).astype(jnp.bfloat16)
    query_rows = jnp.dot(normed, w_query, preferred_element_type=jnp.float32).astype(jnp.bfloat16)
    rows_of_keys = jnp.dot(normed, w_key, preferred_element_type=jnp.float32).astype(jnp.bfloat16)
    rows_of_values = jnp.dot(normed, value_weight, preferred_element_type=jnp.float32).astype(
        jnp.bfloat16
    )
    reach = -(-WINDOW_TOKENS // tok_rows)
    earlier = []
    for distance in range(reach, 0, -1):
        earlier.append(shifted_2((rows_of_keys, rows_of_values), "ctx", distance))
    all_keys = jnp.concatenate([pair[0] for pair in earlier] + [rows_of_keys], axis=0)
    all_values = jnp.concatenate([pair[1] for pair in earlier] + [rows_of_values], axis=0)
    key_count = all_keys.shape[0]
    query_heads = query_rows.reshape(tok_rows, local_kv, group_count_heads, HEAD_SIZE)
    key_heads = all_keys.reshape(key_count, local_kv, HEAD_SIZE)
    value_heads = all_values.reshape(key_count, local_kv, HEAD_SIZE)
    scores = (
        jnp.einsum("rkgd,lkd->kgrl", query_heads, key_heads, preferred_element_type=jnp.float32)
        * SCORE_SCALE
    )
    query_pos = position * tok_rows + jnp.arange(tok_rows, dtype=jnp.int32)[:, None]
    key_pos = (position - reach) * tok_rows + jnp.arange(key_count, dtype=jnp.int32)[None, :]
    allowed = (key_pos <= query_pos) & (query_pos - key_pos < WINDOW_TOKENS) & (key_pos >= 0)
    scores = jnp.where(allowed, scores, -jnp.inf)
    row_max = jnp.max(scores, axis=-1, keepdims=True)
    lifted = jnp.exp(scores - row_max)
    prob_rows = (lifted / jnp.sum(lifted, axis=-1, keepdims=True)).astype(jnp.bfloat16)
    attended = jnp.einsum(
        "kgrl,lkd->rkgd", prob_rows, value_heads, preferred_element_type=jnp.float32
    )
    attended = attended.astype(jnp.bfloat16).reshape(tok_rows, local_heads * HEAD_SIZE)
    gate_value, gate_slope, penalty_term = hard_concrete(mask_logit, noise_draw)
    gate_columns = jnp.repeat(gate_value, HEAD_SIZE)
    gated = (attended.astype(jnp.float32) * gate_columns[None, :]).astype(jnp.bfloat16)
    partial_out = jnp.dot(gated, w_out, preferred_element_type=jnp.float32)
    layer_out = sum_at_owner(partial_out.astype(jnp.bfloat16), "head", 1).astype(jnp.bfloat16)
    local_sum = lax.dot_general(attended, cotangent, TRANSPOSED, preferred_element_type=jnp.float32)
    summed = lax.psum_scatter(
        local_sum.astype(jnp.bfloat16), "ctx", scatter_dimension=1, tiled=True
    ).astype(jnp.float32)
    grad_out_proj = summed * gate_columns[:, None] * inv_root
    through = lax.dot_general(
        cotangent, w_out, (((1,), (1,)), ((), ())), preferred_element_type=jnp.float32
    )
    head_terms = jnp.sum(
        (through * attended.astype(jnp.float32)).reshape(tok_rows, local_heads, HEAD_SIZE),
        axis=(0, 2),
    )
    gate_product = of_everyone(head_terms, "ctx")
    grad_logit = gate_product * inv_root * gate_slope + penalty_term
    return (layer_out, grad_logit, grad_out_proj)


def solution(mesh):
    return jax.shard_map(
        body,
        mesh=mesh,
        in_specs=(
            P("ctx", None),
            P(),
            P(None, "head"),
            P(None, "head"),
            P(None, "head"),
            P("head", None),
            P("head"),
            P("head"),
            P("ctx", None),
        ),
        out_specs=(P("ctx", "head"), P("head"), P("head", "ctx")),
        check_vma=False,
    )
```

profile of v0, /device:TPU:0, one launch (start us, length us, event | category | flops | bytes accessed | tf_op | source)
XLA Modules:
  0.0 189.4 jit_solution(16246812598879664370)
XLA Ops:
  7.2 0.9 convert_element_type.46
  8.1 4.2 %fusion.1 = f32[512]{0:T(512)S(1)} fusion(bf16[512,5376]{1,0:T(8,128)(2,1)} %param.9), kind=kLoop, calls=%fused_computation.6 | loop fusion | flops 8257024 | bytes 5507072 | tf_op jit(solution)/shard_map/reduce_sum | solution.py:68
  12.3 1.7 convolution_convert_fusion.3
  14.0 5.2 %collective-permute-start.2 = (bf16[512,256]{1,0:T(8,128)(2,1)S(1)}, bf16[512,256]{1,0:T(8,128)(2,1)S(1)}, u32[]{:S(2)}, u32[]{:S(2)}) collective-permute-start(bf16[512,256]{1,0:T(8,128)(2,1)S(1)} %convolution_convert_fusion.3), channel_id=1, source_target_pairs={{0,16},{8,24},{16,32},{24,40},{32,48},{40,56},{48,64},{56,72},{64,... | collective-permute-start | bytes 786440 | tf_op jit(solution)/shard_map/ppermute | solution.py:24
  19.3 2.6 %collective-permute-start.3 = (bf16[512,256]{1,0:T(8,128)(2,1)S(1)}, bf16[512,256]{1,0:T(8,128)(2,1)S(1)}, u32[]{:S(2)}, u32[]{:S(2)}) collective-permute-start(bf16[512,256]{1,0:T(8,128)(2,1)S(1)} %convolution_convert_fusion.3), channel_id=1, source_target_pairs={{0,8},{8,16},{16,24},{24,32},{32,40},{40,48},{48,56},{56,64},{64,7... | collective-permute-start | bytes 786440 | tf_op jit(solution)/shard_map/ppermute | solution.py:24
  21.9 1.7 convolution_convert_fusion.4
  23.6 4.7 %collective-permute-start = (bf16[512,256]{1,0:T(8,128)(2,1)S(1)}, bf16[512,256]{1,0:T(8,128)(2,1)S(1)}, u32[]{:S(2)}, u32[]{:S(2)}) collective-permute-start(bf16[512,256]{1,0:T(8,128)(2,1)S(1)} %convolution_convert_fusion.4), channel_id=1, source_target_pairs={{0,16},{8,24},{16,32},{24,40},{32,48},{40,56},{48,64},{56,72},{64,... | collective-permute-start | bytes 786440 | tf_op jit(solution)/shard_map/ppermute | solution.py:24
  28.3 3.5 %collective-permute-start.1 = (bf16[512,256]{1,0:T(8,128)(2,1)S(1)}, bf16[512,256]{1,0:T(8,128)(2,1)S(1)}, u32[]{:S(2)}, u32[]{:S(2)}) collective-permute-start(bf16[512,256]{1,0:T(8,128)(2,1)S(1)} %convolution_convert_fusion.4), channel_id=1, source_target_pairs={{0,8},{8,16},{16,24},{24,32},{32,40},{40,48},{48,56},{56,64},{64,7... | collective-permute-start | bytes 786440 | tf_op jit(solution)/shard_map/ppermute | solution.py:24
  31.8 8.1 %convolution_convert_fusion.2 = bf16[512,512]{0,1:T(8,128)(2,1)} fusion(bf16[5376,512]{1,0:T(8,128)(2,1)} %param.11, bf16[512,5376]{1,0:T(8,128)(2,1)} %param.9, f32[5376]{0:T(1024)} %copy-done.3, f32[512]{0:T(512)S(1)} %add_rsqrt_fusion), kind=kOutput, calls=%fused_computation.23 | convolution fusion | flops 2829844480 | bytes 11557888 | tf_op jit(solution)/shard_map/dot_general | solution.py:72
  40.0 1.2 fusion.10
  41.4 0.3 collective-permute-done.1
  41.8 0.3 copy.40
  42.1 10.1 %fusion.31 = (f32[2,2,512]{2,1,0:T(2,128)S(1)}, f32[2,2,512,1536]{2,3,1,0:T(8,128)}) fusion(pred[512,1536]{0,1:T(8,128)(4,1)S(1)} %fusion.10, bf16[512,2,2,128]{0,3,2,1:T(8,128)(2,1)} %bitcast.44, bf16[1536,2,128,1]{2,1,0,3:T(2,128)(2,1)S(1)} %bitcast.40), kind=kOutput, calls=%fused_computation.48 | convolution fusion | flops 817890816 | bytes 14688256 | tf_op jit(solution)/shard_map/sub | solution.py:96
  52.2 5.6 %fusion.13 = bf16[2,128,2,512]{3,1,2,0:T(8,128)(2,1)S(1)} fusion(bf16[1536,2,128,1]{0,2,3,1:T(8,128)(2,1)S(1)} %bitcast.41, f32[2,2,512,1536]{2,3,1,0:T(8,128)} %get-tuple-element.6, f32[2,2,512]{2,1,0:T(2,128)S(1)} %get-tuple-element.5), kind=kOutput, calls=%fused_computation.22 | convolution fusion | flops 811859968 | bytes 13901824 | tf_op jit(solution)/shard_map/kgrl,lkd->rkgd/dot_general | solution.py:98
  57.8 8.6 %convolution_convert_fusion = bf16[512,5376]{0,1:T(8,128)(2,1)} fusion(bf16[512,512]{0,1:T(8,128)(2,1)S(1)} %bitcast.42, bf16[512,5376]{1,0:T(8,128)(2,1)} %param.17), kind=kOutput, calls=%fused_computation.10 | convolution fusion | flops 2821324800 | bytes 11534336 | tf_op jit(solution)/shard_map/dot_general | solution.py:107
  66.4 0.2 copy.33
  66.7 7.2 %fusion.14 = f32[512]{0:T(512)S(1)} fusion(bf16[512,512]{1,0:T(8,128)(2,1)S(1)} %copy.33, bf16[512,5376]{1,0:T(8,128)(2,1)} %param.17, bf16[512,5376]{1,0:T(8,128)(2,1)} %param.14), kind=kOutput, calls=%fused_computation.24 | convolution fusion | flops 2819358208 | bytes 11536384 | tf_op jit(solution)/shard_map/dot_general | solution.py:112
  74.0 15.2 %all_to_all.11 = f32[16,1,4]{2,1,0:T(1,128)S(1)} all-to-all(f32[16,1,4]{2,1,0:T(1,128)S(1)} %broadcast_in_dim.25), channel_id=1, replica_groups=mesh['ctx'=16,'head'=8] {'ctx'}, dimensions={0} | all-to-all | bytes 512 | tf_op jit(solution)/shard_map/all_to_all | solution.py:40
  89.3 0.5 multiply_add_fusion
  89.9 7.4 %convolution_convert_fusion.1 = bf16[512,5376]{1,0:T(8,128)(2,1)} fusion(bf16[512,5376]{1,0:T(8,128)(2,1)} %param.14, bf16[512,512]{1,0:T(8,128)(2,1)S(1)} %copy.33, f32[512]{0:T(512)S(1)} %broadcast_bitcast_fusion), kind=kOutput, calls=%fused_computation.11 | convolution fusion | flops 2822111232 | bytes 11536384 | tf_op jit(solution)/shard_map/dot_general | solution.py:105
  97.3 8.3 %copy.34 = bf16[512,5376]{0,1:T(8,128)(2,1)} copy(bf16[512,5376]{1,0:T(8,128)(2,1)} %convolution_convert_fusion.1) | data formatting | bytes 11010048 | tf_op jit(solution)/shard_map/convert_element_type | solution.py:106
  105.6 70.6 %all_to_all.12 = bf16[8,512,672]{1,2,0:T(8,128)(2,1)} all-to-all(bf16[8,512,672]{1,2,0:T(8,128)(2,1)} %bitcast.39), channel_id=1, replica_groups=mesh['ctx'=16,'head'=8] {'head'}, dimensions={0} | all-to-all | bytes 11010048 | tf_op jit(solution)/shard_map/all_to_all | solution.py:34
  176.2 4.4 %reduce_sum.57 = bf16[512,672]{0,1:T(8,128)(2,1)} reduce(bf16[8,512,672]{1,2,0:T(8,128)(2,1)} %all_to_all.12, bf16[]{:T(256)} %constant.44.clone.1), dimensions={0}, to_apply=%region_3.4 | reduce | flops 2408448 | bytes 6193154 | tf_op jit(solution)/shard_map/reduce_sum | solution.py:35
  180.6 1.9 %multiply_multiply_fusion = f32[512,336]{0,1:T(8,128)} fusion(bf16[512,336]{0,1:T(8,128)(2,1)} %reduce-scatter.2.cloned.1.call-done, f32[512]{0:T(512)S(1)} %broadcast_bitcast_fusion), kind=kLoop, calls=%fused_computation.33 | loop fusion | flops 516096 | bytes 1034240 | tf_op jit(solution)/shard_map/mul | solution.py:111
  (32 shorter events, 0.7 us)
Async XLA Ops:
  7.2 5.1 %copy-start = (bf16[5376,256]{1,0:T(8,128)(2,1)S(1)}, bf16[5376,256]{1,0:T(8,128)(2,1)}, u32[]{:S(2)}) copy-start(bf16[5376,256]{1,0:T(8,128)(2,1)} %param.12) | copy-start | bytes 8257540
  7.2 173.4 %reduce-scatter.2.cloned.1.call-start = ((), (), s32[]{:S(2)}) async-start(), calls=%async_computation.3 | async-start | bytes 5849088 | tf_op jit(solution)/shard_map/reduce_scatter | solution.py:108
  7.2 5.1 %copy-start.2 = (bf16[512,5376]{1,0:T(8,128)(2,1)S(1)}, bf16[512,5376]{1,0:T(8,128)(2,1)}, u32[]{:S(2)}) copy-start(bf16[512,5376]{1,0:T(8,128)(2,1)} %param.9) | copy-start | bytes 16515076
  8.1 13.8 %copy-start.3 = (f32[5376]{0:T(1024)}, f32[5376]{0:T(1024)S(1)}, u32[]{:S(2)}) copy-start(f32[5376]{0:T(1024)S(1)} %convert_element_type.46) | copy-start | bytes 64516
  12.3 9.6 %copy-start.6 = (bf16[5376,256]{1,0:T(8,128)(2,1)S(1)}, bf16[5376,256]{1,0:T(8,128)(2,1)}, u32[]{:S(2)}) copy-start(bf16[5376,256]{1,0:T(8,128)(2,1)} %param.13) | copy-start | bytes 8257540
  14.0 27.1 %collective-permute-start.2 = (bf16[512,256]{1,0:T(8,128)(2,1)S(1)}, bf16[512,256]{1,0:T(8,128)(2,1)S(1)}, u32[]{:S(2)}, u32[]{:S(2)}) collective-permute-start(bf16[512,256]{1,0:T(8,128)(2,1)S(1)} %convolution_convert_fusion.3), channel_id=1, source_target_pairs={{0,16},{8,24},{16,32},{24,40},{32,48},{40,56},{48,64},{56,72},{64,... | collective-permute-start | bytes 786440 | tf_op jit(solution)/shard_map/ppermute | solution.py:24
  19.3 21.9 %collective-permute-start.3 = (bf16[512,256]{1,0:T(8,128)(2,1)S(1)}, bf16[512,256]{1,0:T(8,128)(2,1)S(1)}, u32[]{:S(2)}, u32[]{:S(2)}) collective-permute-start(bf16[512,256]{1,0:T(8,128)(2,1)S(1)} %convolution_convert_fusion.3), channel_id=1, source_target_pairs={{0,8},{8,16},{16,24},{24,32},{32,40},{40,48},{48,56},{56,64},{64,7... | collective-permute-start | bytes 786440 | tf_op jit(solution)/shard_map/ppermute | solution.py:24
  23.6 17.8 %collective-permute-start = (bf16[512,256]{1,0:T(8,128)(2,1)S(1)}, bf16[512,256]{1,0:T(8,128)(2,1)S(1)}, u32[]{:S(2)}, u32[]{:S(2)}) collective-permute-start(bf16[512,256]{1,0:T(8,128)(2,1)S(1)} %convolution_convert_fusion.4), channel_id=1, source_target_pairs={{0,16},{8,24},{16,32},{24,40},{32,48},{40,56},{48,64},{56,72},{64,... | collective-permute-start | bytes 786440 | tf_op jit(solution)/shard_map/ppermute | solution.py:24
  28.3 13.5 %collective-permute-start.1 = (bf16[512,256]{1,0:T(8,128)(2,1)S(1)}, bf16[512,256]{1,0:T(8,128)(2,1)S(1)}, u32[]{:S(2)}, u32[]{:S(2)}) collective-permute-start(bf16[512,256]{1,0:T(8,128)(2,1)S(1)} %convolution_convert_fusion.4), channel_id=1, source_target_pairs={{0,8},{8,16},{16,24},{24,32},{32,40},{40,48},{48,56},{56,64},{64,7... | collective-permute-start | bytes 786440 | tf_op jit(solution)/shard_map/ppermute | solution.py:24
  66.6 22.6 %copy-start.4 = (f32[4]{0:T(128)S(1)}, f32[4]{0:T(128)}, u32[]{:S(2)}) copy-start(f32[4]{0:T(128)} %param.15) | copy-start | bytes 52
  66.7 22.6 %copy-start.5 = (f32[4]{0:T(128)S(1)}, f32[4]{0:T(128)}, u32[]{:S(2)}) copy-start(f32[4]{0:T(128)} %param.16) | copy-start | bytes 52
  105.6 76.9 %copy-start.1 = (bf16[5376,256]{1,0:T(8,128)(2,1)S(1)}, bf16[5376,256]{1,0:T(8,128)(2,1)}, u32[]{:S(2)}) copy-start(bf16[5376,256]{1,0:T(8,128)(2,1)} %param.12) | copy-start | bytes 8257540
Sparse Core Ops, SparseCore 0:
  66.5 82.5 reduce-scatter.1
where the time goes:
time: 190 us; the launch traced here: 189 us
  blocking collectives  85.8 us (45%)
  matrix products  50.5 us (27%)
  starting transfers between devices  16 us (8%)
  between operations  14.3 us (8%)
  other arithmetic  13.3 us (7%)
  local copies, waits for them, and re-layouts  9.11 us (5%)
    all_to_all x1, blocking collectives, sum_at_owner(): lax.all_to_all(cut_along(value, dim, length), axis, 0, 0, tiled=True)  70.6 us
    ppermute x4, starting transfers between devices, shifted_2(): lax.ppermute(value, axis, [(source, source + steps) for source in range(f...  16 us
    all_to_all x1, blocking collectives, copy_for_each(): return lax.all_to_all(copies, axis, split_axis=0, concat_axis=0, tiled=True)  15.2 us
    sub x1, matrix products, body(): lifted = jnp.exp(scores - row_max)  10.1 us
    dot_general x1, matrix products, body(): lax.dot_general(attended, cotangent, TRANSPOSED, preferred_element_type=j...  8.63 us
    convert_element_type x1, local copies, waits for them, and re-layouts, body(): partial_out.astype(jnp.bfloat16)  8.31 us
    dot_general x1, matrix products, body(): jnp.dot(normed, w_query, preferred_element_type=jnp.float32)  8.14 us
    dot_general x1, matrix products, body(): partial_out = jnp.dot(gated, w_out, preferred_element_type=jnp.float32)  7.4 us
  transfers between devices with their start and end apart: 5, of which 1 were waited for; matrix products, arithmetic and copies ran while one was open for 21% of the time, Pallas kernels for 0%

commit v1 on v0

--- a/solution.py
+++ b/solution.py
@@ -1,8 +1,11 @@
+import functools
 import math
 
 import jax
 import jax.numpy as jnp
 from jax import lax
+from jax.experimental import pallas as pl
+from jax.experimental.pallas import tpu as pltpu
 from jax.sharding import PartitionSpec as P
 
 HEAD_SIZE = 128
@@ -18,30 +21,305 @@
 TRANSPOSED = (((0,), (0,)), ((), ()))
 
 
+MESH = pl.DeviceIdType.MESH
+BF16 = jnp.bfloat16
+F32 = jnp.float32
+GRAD_ROWS = 336
+OUT_ROWS = 672
+HALF_OUT = 336
+SPLIT = 176
+
+
+class Links:
+    def __init__(self, send, recv):
+        self.send, self.recv, self.count, self.open = send, recv, 0, []
+
+    def start(self, source, target, device):
+        copy = pltpu.make_async_remote_copy(
+            src_ref=source,
+            dst_ref=target,
+            send_sem=self.send.at[self.count],
+            recv_sem=self.recv.at[self.count],
+            device_id=device,
+            device_id_type=MESH,
+        )
+        self.count += 1
+        copy.start()
+        self.open.append(copy)
+        return copy
+
+    def finish(self):
+        for copy in self.open:
+            copy.wait_send()
+
+
+def wide(value):
+    return value.astype(F32)
+
+
+def reduce_kernel(
+    att, gated, cot_t, wout_t, grad_out, layer_out, gate_out,
+    grad, grad_in, line, line_in, out, out_core, out_in, gate_acc, gate_in, send, recv,
+):
+    ctx, head = lax.axis_index("ctx"), lax.axis_index("head")
+    px, py = ctx // 4, ctx % 4
+    pz, core = head // 2, head % 2
+
+    def at_x(step):
+        return ((px + step) % 4 * 4 + py, head)
+
+    def at_y(step):
+        return (px * 4 + (py + step) % 4, head)
+
+    def at_z(step):
+        return (ctx, (pz + step) % 4 * 2 + core)
+
+    sibling = (ctx, pz * 2 + (1 - core))
+    places = {"x": (px, at_x), "y": (py, at_y)}
+    peers = [at(step) for at in (at_x, at_y) for step in (1, 2, 3)] + [at_z(1), at_z(3), sibling]
+    barrier = pltpu.get_barrier_semaphore()
+    for peer in peers:
+        pl.semaphore_signal(barrier, inc=1, device_id=peer, device_id_type=MESH)
+    pl.semaphore_wait(barrier, len(peers))
+    links = Links(send, recv)
+
+    def block_of(number, first, target, half):
+        if first == "y":
+            return grad.at[number, pl.ds(2 * half, 2), target]
+        return grad.at[number, target, pl.ds(2 * half, 2)]
+
+    firsts = ["y", "x", "y", "x"]
+    gate_acc[...] = jnp.zeros_like(gate_acc)
+    gate_in[0] = jnp.zeros((8, 128), F32)
+
+    def grad_pair(pair):
+        def chunk(index, carry):
+            rows = pl.ds(pl.multiple_of(index * GRAD_ROWS, 16), GRAD_ROWS)
+            product = jnp.dot(
+                cot_t[rows, :], att[:, 256 * pair : 256 * pair + 256], preferred_element_type=F32
+            )
+            for side in range(2):
+                number = 2 * pair + side
+                mine = product[:, 128 * side : 128 * side + 128]
+                grad[number, index // 4, index % 4] = mine.astype(BF16)
+                weighed = mine * wide(wout_t[rows, 128 * number : 128 * number + 128])
+                gate_acc[number] += jnp.sum(weighed.reshape(GRAD_ROWS // 8, 8, 128), axis=0)
+            return carry
+
+        lax.fori_loop(0, 16, chunk, 0)
+
+    stage1 = {}
+
+    def send_first(number):
+        first = firsts[number]
+        place, at = places[first]
+        far, after, before = (place + 2) % 4, (place + 1) % 4, (place + 3) % 4
+        box = grad_in.at[number]
+        stage1[number] = [
+            links.start(block_of(number, first, far, 0), box.at[0], at(1)),
+            links.start(block_of(number, first, far, 1), box.at[1], at(3)),
+            links.start(block_of(number, first, before, 0), box.at[2], at(3)),
+            links.start(block_of(number, first, after, 1), box.at[3], at(1)),
+        ]
+
+    def relay_first(number):
+        first = firsts[number]
+        place, at = places[first]
+        after, before = (place + 1) % 4, (place + 3) % 4
+        box = grad_in.at[number]
+        for slot, target, half, step in ((0, after, 0, 1), (1, before, 1, 3)):
+            stage1[number][slot].wait_recv()
+            box[slot] = (wide(box[slot]) + wide(block_of(number, first, target, half)[...])).astype(BF16)
+            stage1[number].append(links.start(box.at[slot], box.at[4 + slot], at(step)))
+
+    def end_first(number):
+        first = firsts[number]
+        place, _ = places[first]
+        box = grad_in.at[number]
+        for half in range(2):
+            stage1[number][2 + half].wait_recv()
+            stage1[number][4 + half].wait_recv()
+            total = wide(block_of(number, first, place, half)[...]) + wide(box[2 + half]) + wide(box[4 + half])
+            line[number, pl.ds(2 * half, 2)] = total.astype(BF16)
+
+    stage2 = {}
+    cuts = (pl.ds(0, SPLIT), pl.ds(SPLIT, GRAD_ROWS - SPLIT))
+    sizes = (pl.ds(0, SPLIT), pl.ds(0, GRAD_ROWS - SPLIT))
+
+    def send_second(number):
+        place, at = places["x" if firsts[number] == "y" else "y"]
+        far, after, before = (place + 2) % 4, (place + 1) % 4, (place + 3) % 4
+        mine, box = line.at[number], line_in.at[number]
+        stage2[number] = [
+            links.start(mine.at[far, cuts[0]], box.at[0, sizes[0]], at(1)),
+            links.start(mine.at[far, cuts[1]], box.at[1, sizes[1]], at(3)),
+            links.start(mine.at[before, cuts[0]], box.at[2, sizes[0]], at(3)),
+            links.start(mine.at[after, cuts[1]], box.at[3, sizes[1]], at(1)),
+        ]
+
+    def relay_second(number):
+        place, at = places["x" if firsts[number] == "y" else "y"]
+        after, before = (place + 1) % 4, (place + 3) % 4
+        mine, box = line.at[number], line_in.at[number]
+        for slot, target, step in ((0, after, 1), (1, before, 3)):
+            stage2[number][slot].wait_recv()
+            part = box.at[slot, sizes[slot]]
+            part[...] = (wide(part[...]) + wide(mine[target, cuts[slot]])).astype(BF16)
+            stage2[number].append(links.start(part, box.at[4 + slot, sizes[slot]], at(step)))
+
+    def end_second(number):
+        place, _ = places["x" if firsts[number] == "y" else "y"]
+        mine, box = line.at[number], line_in.at[number]
+        for half in range(2):
+            stage2[number][2 + half].wait_recv()
+            stage2[number][4 + half].wait_recv()
+            grad_out[number, cuts[half]] = (
+                wide(mine[place, cuts[half]])
+                + wide(box[2 + half, sizes[half]])
+                + wide(box[4 + half, sizes[half]])
+            )
+
+    def out_part(which, place):
+        def piece(index, carry):
+            row = pl.multiple_of(index * 112, 16)
+            source = pl.multiple_of((place * 2 + which) * OUT_ROWS + index * 112, 16)
+            product = lax.dot_general(
+                wout_t[pl.ds(source, 112), :], gated[...], (((1,), (1,)), ((), ())),
+                preferred_element_type=F32,
+            )
+            out[which, place, pl.ds(row, 112), :] = product.astype(BF16)
+            return carry
+
+        lax.fori_loop(0, OUT_ROWS // 112, piece, 0)
+
+    grad_pair(0)
+    send_first(0)
+    send_first(1)
+    order = [(pz + step) % 4 for step in (2, 1, 3, 0)]
+    across = []
+    for place in order[:2]:
+        out_part(1 - core, place)
+        across.append(links.start(out.at[1 - core, place], out_core.at[place], sibling))
+    grad_pair(1)
+    send_first(2)
+    send_first(3)
+    for place in order[2:]:
+        out_part(1 - core, place)
+        across.append(links.start(out.at[1 - core, place], out_core.at[place], sibling))
+
+    for number in range(4):
+        gate_in[0, pl.ds(number, 1)] = jnp.sum(gate_acc[number], axis=0, keepdims=True)
+    gate_y = [links.start(gate_in.at[0], gate_in.at[step], at_y(step)) for step in (1, 2, 3)]
+    relay_first(0)
+    relay_first(1)
+    for place in order:
+        out_part(core, place)
+
+    def add_core(index):
+        across[index].wait_recv()
+        place = order[index]
+
+        def piece(step, carry):
+            rows = pl.ds(pl.multiple_of(step * 112, 16), 112)
+            out[core, place, rows] = (wide(out[core, place, rows]) + wide(out_core[place, rows])).astype(BF16)
+            return carry
+
+        lax.fori_loop(0, OUT_ROWS // 112, piece, 0)
+
+    far, after, before = order[0], order[1], order[2]
+    upper, lower = pl.ds(0, HALF_OUT), pl.ds(HALF_OUT, HALF_OUT)
+    mine = out.at[core]
+    add_core(0)
+    ring = [
+        links.start(mine.at[far, upper], out_in.at[0], at_z(1)),
+        links.start(mine.at[far, lower], out_in.at[1], at_z(3)),
+    ]
+    add_core(1)
+    add_core(2)
+    ring += [
+        links.start(mine.at[before, upper], out_in.at[2], at_z(3)),
+        links.start(mine.at[after, lower], out_in.at[3], at_z(1)),
+    ]
+    relay_first(2)
+    relay_first(3)
+    add_core(3)
+    for copy in gate_y:
+        copy.wait_recv()
+    gate_in[4] = gate_in[0] + gate_in[1] + gate_in[2] + gate_in[3]
+    gate_x = [links.start(gate_in.at[4], gate_in.at[4 + step], at_x(step)) for step in (1, 2, 3)]
+
+    for slot, target, rows, step in ((0, after, 0, 1), (1, before, HALF_OUT, 3)):
+        ring[slot].wait_recv()
+
+        def piece(index, carry, slot=slot, target=target, rows=rows):
+            here = pl.ds(pl.multiple_of(index * 112, 16), 112)
+            there = pl.ds(pl.multiple_of(index * 112 + rows, 16), 112)
+            out_in[slot, here] = (wide(out_in[slot, here]) + wide(out[core, target, there])).astype(BF16)
+            return carry
+
+        lax.fori_loop(0, HALF_OUT // 112, piece, 0)
+        ring.append(links.start(out_in.at[slot], out_in.at[4 + slot], at_z(step)))
+
+    for number in range(4):
+        end_first(number)
+        send_second(number)
+    for copy in gate_x:
+        copy.wait_recv()
+    gate_out[...] = gate_in[4] + gate_in[5] + gate_in[6] + gate_in[7]
+    for number in range(4):
+        relay_second(number)
+    for half in range(2):
+        ring[2 + half].wait_recv()
+        ring[4 + half].wait_recv()
+
+        def piece(index, carry, half=half):
+            here = pl.ds(pl.multiple_of(index * 112, 16), 112)
+            there = pl.ds(pl.multiple_of(index * 112 + half * HALF_OUT, 16), 112)
+            total = wide(out[core, pz, there]) + wide(out_in[2 + half, here]) + wide(out_in[4 + half, here])
+            layer_out[there, :] = total.astype(BF16)
+            return carry
+
+        lax.fori_loop(0, HALF_OUT // 112, piece, 0)
+    for number in range(4):
+        end_second(number)
+    links.finish()
+
+
+def reduce_all(attended, gated, cot_t, wout_t):
+    tokens = attended.shape[0]
+    vmem = pl.BlockSpec(memory_space=pltpu.VMEM)
+    return pl.pallas_call(
+        reduce_kernel,
+        out_shape=(
+            jax.ShapeDtypeStruct((4, GRAD_ROWS, 128), F32),
+            jax.ShapeDtypeStruct((OUT_ROWS, tokens), BF16),
+            jax.ShapeDtypeStruct((8, 128), F32),
+        ),
+        in_specs=[vmem] * 4,
+        out_specs=(vmem,) * 3,
+        scratch_shapes=[
+            pltpu.VMEM((4, 4, 4, GRAD_ROWS, 128), BF16),
+            pltpu.VMEM((4, 6, 2, GRAD_ROWS, 128), BF16),
+            pltpu.VMEM((4, 4, GRAD_ROWS, 128), BF16),
+            pltpu.VMEM((4, 6, SPLIT, 128), BF16),
+            pltpu.VMEM((2, 4, OUT_ROWS, tokens), BF16),
+            pltpu.VMEM((4, OUT_ROWS, tokens), BF16),
+            pltpu.VMEM((6, HALF_OUT, tokens), BF16),
+            pltpu.VMEM((4, 8, 128), F32),
+            pltpu.VMEM((8, 8, 128), F32),
+            pltpu.SemaphoreType.DMA((64,)),
+            pltpu.SemaphoreType.DMA((64,)),
+        ],
+        compiler_params=pltpu.CompilerParams(
+            collective_id=0, has_side_effects=True, vmem_limit_bytes=56 * 2**20
+        ),
+    )(attended, gated, cot_t, wout_t)
+
+
 def shifted_2(value, axis, steps):
     count = lax.axis_size(axis)
     first, last = (max(0, -steps), min(count, count - steps))
     return lax.ppermute(value, axis, [(source, source + steps) for source in range(first, last)])
-
-
-def cut_along(value, dim, length):
-    before, after = (value.shape[:dim], value.shape[dim + 1 :])
-    return jnp.moveaxis(value.reshape(*before, length, -1, *after), dim, 0)
-
-
-def sum_at_owner(value, axis, dim):
-    length = lax.axis_size(axis)
-    parts = lax.all_to_all(cut_along(value, dim, length), axis, 0, 0, tiled=True)
-    return jnp.sum(parts.astype(jnp.float32), axis=0)
-
-
-def copy_for_each(value, axis):
-    copies = jnp.broadcast_to(value, (lax.axis_size(axis), *value.shape))
-    return lax.all_to_all(copies, axis, split_axis=0, concat_axis=0, tiled=True)
-
-
-def of_everyone(value, axis):
-    return copy_for_each(value, axis).sum(axis=0)
 
 
 def hard_concrete(mask_logit, noise_draw):
@@ -102,21 +380,11 @@
     gate_value, gate_slope, penalty_term = hard_concrete(mask_logit, noise_draw)
     gate_columns = jnp.repeat(gate_value, HEAD_SIZE)
     gated = (attended.astype(jnp.float32) * gate_columns[None, :]).astype(jnp.bfloat16)
-    partial_out = jnp.dot(gated, w_out, preferred_element_type=jnp.float32)
-    layer_out = sum_at_owner(partial_out.astype(jnp.bfloat16), "head", 1).astype(jnp.bfloat16)
-    local_sum = lax.dot_general(attended, cotangent, TRANSPOSED, preferred_element_type=jnp.float32)
-    summed = lax.psum_scatter(
-        local_sum.astype(jnp.bfloat16), "ctx", scatter_dimension=1, tiled=True
-    ).astype(jnp.float32)
+    grad_t, out_t, gate_rows = reduce_all(attended, gated, cotangent.T, w_out.T)
+    layer_out = out_t.T
+    summed = jnp.moveaxis(grad_t, 1, 2).reshape(local_heads * HEAD_SIZE, grad_t.shape[1])
     grad_out_proj = summed * gate_columns[:, None] * inv_root
-    through = lax.dot_general(
-        cotangent, w_out, (((1,), (1,)), ((), ())), preferred_element_type=jnp.float32
-    )
-    head_terms = jnp.sum(
-        (through * attended.astype(jnp.float32)).reshape(tok_rows, local_heads, HEAD_SIZE),
-        axis=(0, 2),
-    )
-    gate_product = of_everyone(head_terms, "ctx")
+    gate_product = jnp.sum(gate_rows[:local_heads], axis=1)
     grad_logit = gate_product * inv_root * gate_slope + penalty_term
     return (layer_out, grad_logit, grad_out_proj)
 

time: 190 us -> 143 us (0.75)
  blocking collectives: 85.8 us -> 0 us
  Pallas kernels: 0 us -> 57.7 us
  matrix products: 50.5 us -> 30 us
  local copies, waits for them, and re-layouts: 9.11 us -> 23 us
  between operations: 14.3 us -> 0.76 us
    all_to_all x2 -> x0, blocking collectives: 85.8 us -> none  [the longest x1 70.6 us: sum_at_owner(): lax.all_to_all(cut_along(value, dim, length), axis, 0, 0, tiled=True)]
    pallas_call x0 -> x1, Pallas kernels: none -> 57.7 us  [reduce_all(): pl.pallas_call(reduce_kernel, out_shape=(jax.ShapeDtypeStruct((4, GRAD_RO...]
    dot_general x3 -> x0, matrix products: 23.3 us -> none  [the longest x1 8.63 us: body(): lax.dot_general(attended, cotangent, TRANSPOSED, preferred_element_type=j...]
    unnamed x14 -> x21, local copies, waits for them, and re-layouts: 0.04 us -> 19.3 us
    convert_element_type x1 -> x0, local copies, waits for them, and re-layouts: 8.31 us -> none  [body(): partial_out.astype(jnp.bfloat16)]
    reduce_sum x3 -> x1, other arithmetic: 4.54 us -> 0.79 us  [body(): gate_product = jnp.sum(gate_rows[:local_heads], axis=1)]
  transfers between devices with their start and end apart: 5 -> 4, of which waited for: 1 -> 0; matrix products, arithmetic and copies ran while one was open for 21% -> 22% of each run, Pallas kernels for 0% -> 0%
where the time goes in v1:
time: 143 us; the launch traced here: 142 us
  Pallas kernels  57.7 us (40%)
  matrix products  30 us (21%)
  local copies, waits for them, and re-layouts  23 us (16%)
  starting transfers between devices  17.3 us (12%)
  other arithmetic  13.6 us (10%)
    pallas_call x1, Pallas kernels, reduce_all(): pl.pallas_call(reduce_kernel, out_shape=(jax.ShapeDtypeStruct((4, GRAD_RO...  57.7 us
    unnamed x21, local copies, waits for them, and re-layouts  19.3 us
    ppermute x4, starting transfers between devices, shifted_2(): lax.ppermute(value, axis, [(source, source + steps) for source in range(f...  17.3 us
    sub x1, matrix products, body(): lifted = jnp.exp(scores - row_max)  11.3 us
    dot_general x1, matrix products, body(): jnp.dot(normed, w_query, preferred_element_type=jnp.float32)  8.16 us
    dot_general x1, matrix products, body(): jnp.einsum('kgrl,lkd->rkgd', prob_rows, value_heads, preferred_element_ty...  6.37 us
    reduce_sum x1, other arithmetic, body(): moment = jnp.mean(jnp.square(widened), axis=1, keepdims=True)  4.14 us
  transfers between devices with their start and end apart: 4, of which 0 were waited for; matrix products, arithmetic and copies ran while one was open for 22% of the time, Pallas kernels for 0%

profile of v1, /device:TPU:0, one launch (start us, length us, event | category | flops | bytes accessed | tf_op | source)
XLA Modules:
  0.0 142.3 jit_solution(15830828626767011529)
XLA Ops:
  0.7 0.9 convert_element_type.34
  1.5 4.1 %fusion.1 = f32[512]{0:T(512)S(1)} fusion(bf16[512,5376]{1,0:T(8,128)(2,1)} %param.9), kind=kLoop, calls=%fused_computation.6 | loop fusion | flops 8257024 | bytes 5507072 | tf_op jit(solution)/shard_map/reduce_sum | solution.py:346
  5.7 1.7 %convolution_convert_fusion.1 = bf16[512,256]{1,0:T(8,128)(2,1)S(1)} fusion(bf16[5376,256]{1,0:T(8,128)(2,1)S(1)} %copy-done, bf16[512,5376]{1,0:T(8,128)(2,1)S(1)} %copy-done.1, f32[5376]{0:T(1024)S(1)} %convert_element_type.34, f32[512]{0:T(512)S(1)} %add_rsqrt_fusion), kind=kOutput, calls=%fused_computation.20 | convolution fusion | flops 1420427264 | bytes 8543232 | tf_op jit(solution)/shard_map/dot_general | solution.py:351
  7.4 5.2 %collective-permute-start.2 = (bf16[512,256]{1,0:T(8,128)(2,1)S(1)}, bf16[512,256]{1,0:T(8,128)(2,1)S(1)}, u32[]{:S(2)}, u32[]{:S(2)}) collective-permute-start(bf16[512,256]{1,0:T(8,128)(2,1)S(1)} %convolution_convert_fusion.1), channel_id=1, source_target_pairs={{0,16},{8,24},{16,32},{24,40},{32,48},{40,56},{48,64},{56,72},{64,... | collective-permute-start | bytes 786440 | tf_op jit(solution)/shard_map/ppermute | solution.py:322
  12.7 3.3 %collective-permute-start.3 = (bf16[512,256]{1,0:T(8,128)(2,1)S(1)}, bf16[512,256]{1,0:T(8,128)(2,1)}, u32[]{:S(2)}, u32[]{:S(2)}) collective-permute-start(bf16[512,256]{1,0:T(8,128)(2,1)S(1)} %convolution_convert_fusion.1), channel_id=1, source_target_pairs={{0,8},{8,16},{16,24},{24,32},{32,40},{40,48},{48,56},{56,64},{64,7... | collective-permute-start | bytes 786440 | tf_op jit(solution)/shard_map/ppermute | solution.py:322
  16.0 2.5 %convolution_convert_fusion.2 = bf16[512,256]{1,0:T(8,128)(2,1)} fusion(bf16[5376,256]{1,0:T(8,128)(2,1)S(1)} %copy-done.8, bf16[512,5376]{1,0:T(8,128)(2,1)S(1)} %copy-done.1, f32[5376]{0:T(1024)S(1)} %convert_element_type.34, f32[512]{0:T(512)S(1)} %add_rsqrt_fusion), kind=kOutput, calls=%fused_computation.21 | convolution fusion | flops 1420427264 | bytes 8543232 | tf_op jit(solution)/shard_map/dot_general | solution.py:352
  18.4 4.7 %collective-permute-start = (bf16[512,256]{1,0:T(8,128)(2,1)}, bf16[512,256]{1,0:T(8,128)(2,1)}, u32[]{:S(2)}, u32[]{:S(2)}) collective-permute-start(bf16[512,256]{1,0:T(8,128)(2,1)} %convolution_convert_fusion.2), channel_id=1, source_target_pairs={{0,16},{8,24},{16,32},{24,40},{32,48},{40,56},{48,64},{56,72},{64,... | collective-permute-start | bytes 786440 | tf_op jit(solution)/shard_map/ppermute | solution.py:322
  23.1 4.2 %collective-permute-start.1 = (bf16[512,256]{1,0:T(8,128)(2,1)}, bf16[512,256]{1,0:T(8,128)(2,1)}, u32[]{:S(2)}, u32[]{:S(2)}) collective-permute-start(bf16[512,256]{1,0:T(8,128)(2,1)} %convolution_convert_fusion.2), channel_id=1, source_target_pairs={{0,8},{8,16},{16,24},{24,32},{32,40},{40,48},{48,56},{56,64},{64,7... | collective-permute-start | bytes 786440 | tf_op jit(solution)/shard_map/ppermute | solution.py:322
  27.3 8.2 %convolution_convert_fusion = bf16[512,512]{0,1:T(8,128)(2,1)} fusion(bf16[5376,512]{1,0:T(8,128)(2,1)} %param.11, bf16[512,5376]{1,0:T(8,128)(2,1)} %param.9, f32[5376]{0:T(1024)S(1)} %convert_element_type.34, f32[512]{0:T(512)S(1)} %add_rsqrt_fusion), kind=kOutput, calls=%fused_computation.19 | convolution fusion | flops 2829844480 | bytes 11557888 | tf_op jit(solution)/shard_map/dot_general | solution.py:350
  35.4 1.9 %fusion.10 = pred[512,1536]{0,1:T(8,128)(4,1)} fusion(s32[512]{0:T(512)S(1)} %iota_add_fusion.1, s32[1536]{0:T(1024)S(1)} %iota_add_fusion, pred[1536]{0:T(1024)(128)(4,1)S(1)} %broadcast_compare_fusion), kind=kLoop, calls=%fused_computation.16 | loop fusion | flops 3932160 | bytes 796160 | tf_op jit(solution)/shard_map/and | solution.py:371
  37.4 8.3 %copy.24 = bf16[512,5376]{0,1:T(8,128)(2,1)} copy(bf16[512,5376]{1,0:T(8,128)(2,1)} %param.17) | data formatting | bytes 11010048 | tf_op args[8]
  45.7 8.3 %copy.25 = bf16[512,5376]{0,1:T(8,128)(2,1)} copy(bf16[512,5376]{1,0:T(8,128)(2,1)} %param.14) | data formatting | bytes 11010048 | tf_op args[5]
  54.8 1.2 pad_maximum_fusion.1
  55.9 1.1 reshape.48
  57.0 1.2 pad_maximum_fusion
  58.2 1.2 copy.31
  59.4 11.3 %fusion.28 = (f32[2,2,512]{2,1,0:T(2,128)}, f32[2,2,512,1536]{2,3,1,0:T(8,128)}) fusion(pred[512,1536]{0,1:T(8,128)(4,1)} %fusion.10, bf16[512,2,2,128]{0,3,2,1:T(8,128)(2,1)} %bitcast.46, bf16[1536,2,128,1]{2,1,0,3:T(2,128)(2,1)} %bitcast.42), kind=kOutput, calls=%fused_computation.43 | convolution fusion | flops 817890816 | bytes 14688256 | tf_op jit(solution)/shard_map/sub | solution.py:374
  70.7 6.4 %fusion.13 = bf16[2,128,2,512]{3,1,2,0:T(8,128)(2,1)} fusion(bf16[1536,2,128,1]{0,2,3,1:T(8,128)(2,1)S(1)} %bitcast.43, f32[2,2,512,1536]{2,3,1,0:T(8,128)} %get-tuple-element.12, f32[2,2,512]{2,1,0:T(2,128)} %get-tuple-element.11), kind=kOutput, calls=%fused_computation.18 | convolution fusion | flops 811859968 | bytes 13901824 | tf_op jit(solution)/shard_map/kgrl,lkd->rkgd/dot_general | solution.py:376
  77.0 1.3 copy.34.att
  78.3 1.0 multiply_convert_fusion.gated
  79.3 57.7 %shard_map.112 = (f32[4,336,128]{2,1,0:T(8,128)}, bf16[672,512]{1,0:T(8,128)(2,1)}, f32[8,128]{1,0:T(8,128)}) custom-call(bf16[512,512]{1,0:T(8,128)(2,1)} %copy-done.2, bf16[512,512]{1,0:T(8,128)(2,1)} %multiply_convert_fusion.gated, bf16[5376,512]{1,0:T(8,128)(2,1)} %bitcast.40, bf16[5376,512]{1,0:T(8,128)(2,1)} %bitcast.41), custom_call_target="tpu_custom_call" | custom-call | tf_op jit(solution)/shard_map/pallas_call | solution.py:291
  137.0 2.0 %fusion.21 = f32[512,336]{0,1:T(8,128)} fusion(f32[512]{0:T(512)S(1)} %broadcast_bitcast_fusion, f32[4,336,128]{2,1,0:T(8,128)} %get-tuple-element.8), kind=kLoop, calls=%fused_computation.29 | loop fusion | flops 344064 | bytes 1378304 | tf_op jit(solution)/shard_map/mul | solution.py:386
  139.0 0.8 slice_reduce_fusion
  140.3 2.0 %copy.50 = bf16[512,672]{0,1:T(8,128)(2,1)} copy(bf16[512,672]{0,1:T(8,128)(2,1)} %bitcast.44) | data formatting | bytes 1376256
  (29 shorter events, 1.4 us)
Async XLA Ops:
  0.6 5.0 %copy-start = (bf16[5376,256]{1,0:T(8,128)(2,1)S(1)}, bf16[5376,256]{1,0:T(8,128)(2,1)}, u32[]{:S(2)}) copy-start(bf16[5376,256]{1,0:T(8,128)(2,1)} %param.12) | copy-start | bytes 8257540
  0.6 5.0 %copy-start.1 = (bf16[512,5376]{1,0:T(8,128)(2,1)S(1)}, bf16[512,5376]{1,0:T(8,128)(2,1)}, u32[]{:S(2)}) copy-start(bf16[512,5376]{1,0:T(8,128)(2,1)} %param.9) | copy-start | bytes 16515076
  5.7 10.3 %copy-start.8 = (bf16[5376,256]{1,0:T(8,128)(2,1)S(1)}, bf16[5376,256]{1,0:T(8,128)(2,1)}, u32[]{:S(2)}) copy-start(bf16[5376,256]{1,0:T(8,128)(2,1)} %param.13) | copy-start | bytes 8257540
  7.4 11.0 %copy-start.4 = (bf16[512,256]{1,0:T(8,128)(2,1)}, bf16[512,256]{1,0:T(8,128)(2,1)S(1)}, u32[]{:S(2)}) copy-start(bf16[512,256]{1,0:T(8,128)(2,1)S(1)} %convolution_convert_fusion.1) | copy-start | bytes 786436
  7.4 46.6 %collective-permute-start.2 = (bf16[512,256]{1,0:T(8,128)(2,1)S(1)}, bf16[512,256]{1,0:T(8,128)(2,1)S(1)}, u32[]{:S(2)}, u32[]{:S(2)}) collective-permute-start(bf16[512,256]{1,0:T(8,128)(2,1)S(1)} %convolution_convert_fusion.1), channel_id=1, source_target_pairs={{0,16},{8,24},{16,32},{24,40},{32,48},{40,56},{48,64},{56,72},{64,... | collective-permute-start | bytes 786440 | tf_op jit(solution)/shard_map/ppermute | solution.py:322
  12.7 42.1 %collective-permute-start.3 = (bf16[512,256]{1,0:T(8,128)(2,1)S(1)}, bf16[512,256]{1,0:T(8,128)(2,1)}, u32[]{:S(2)}, u32[]{:S(2)}) collective-permute-start(bf16[512,256]{1,0:T(8,128)(2,1)S(1)} %convolution_convert_fusion.1), channel_id=1, source_target_pairs={{0,8},{8,16},{16,24},{24,32},{32,40},{40,48},{48,56},{56,64},{64,7... | collective-permute-start | bytes 786440 | tf_op jit(solution)/shard_map/ppermute | solution.py:322
  18.4 38.6 %collective-permute-start = (bf16[512,256]{1,0:T(8,128)(2,1)}, bf16[512,256]{1,0:T(8,128)(2,1)}, u32[]{:S(2)}, u32[]{:S(2)}) collective-permute-start(bf16[512,256]{1,0:T(8,128)(2,1)} %convolution_convert_fusion.2), channel_id=1, source_target_pairs={{0,16},{8,24},{16,32},{24,40},{32,48},{40,56},{48,64},{56,72},{64,... | collective-permute-start | bytes 786440 | tf_op jit(solution)/shard_map/ppermute | solution.py:322
  23.1 34.0 %collective-permute-start.1 = (bf16[512,256]{1,0:T(8,128)(2,1)}, bf16[512,256]{1,0:T(8,128)(2,1)}, u32[]{:S(2)}, u32[]{:S(2)}) collective-permute-start(bf16[512,256]{1,0:T(8,128)(2,1)} %convolution_convert_fusion.2), channel_id=1, source_target_pairs={{0,8},{8,16},{16,24},{24,32},{32,40},{40,48},{48,56},{56,64},{64,7... | collective-permute-start | bytes 786440 | tf_op jit(solution)/shard_map/ppermute | solution.py:322
  27.3 10.1 %copy-start.6 = (f32[4]{0:T(128)S(1)}, f32[4]{0:T(128)}, u32[]{:S(2)}) copy-start(f32[4]{0:T(128)} %param.15) | copy-start | bytes 52
  27.3 10.1 %copy-start.7 = (f32[4]{0:T(128)S(1)}, f32[4]{0:T(128)}, u32[]{:S(2)}) copy-start(f32[4]{0:T(128)} %param.16) | copy-start | bytes 52
  54.1 0.7 copy-start.5
  59.4 11.3 %copy-start.3 = (bf16[1536,256]{0,1:T(8,128)(2,1)S(1)}, bf16[1536,256]{0,1:T(8,128)(2,1)}, u32[]{:S(2)}) copy-start(bf16[1536,256]{0,1:T(8,128)(2,1)} %copy.31) | copy-start | bytes 2359300
  78.3 1.0 copy-start.2

commit v2 on v1

v2 whole, which is shorter than its diff:
```python
import math

import jax
import jax.numpy as jnp
from jax import lax
from jax.experimental import pallas as pl
from jax.experimental.pallas import tpu as pltpu
from jax.sharding import PartitionSpec as P

HEAD_SIZE = 128


EPSILON = 1e-06
BETA = 2.0 / 3.0
GAMMA = -0.1
ZETA = 1.1
PENALTY = 0.1
SCORE_POWER = 168.0 ** (-0.5) * math.log2(math.e)


MESH = pl.DeviceIdType.MESH
BF16 = jnp.bfloat16
F32 = jnp.float32
GRAD_ROWS = 336
OUT_ROWS = 672
HALF_OUT = 336
SPLIT = 176


class Links:
    def __init__(self, send, recv):
        self.send, self.recv, self.count, self.open = send, recv, 0, []

    def start(self, source, target, device):
        copy = pltpu.make_async_remote_copy(
            src_ref=source,
            dst_ref=target,
            send_sem=self.send.at[self.count],
            recv_sem=self.recv.at[self.count],
            device_id=device,
            device_id_type=MESH,
        )
        self.count += 1
        copy.start()
        self.open.append(copy)
        return copy

    def finish(self):
        for copy in self.open:
            copy.wait_send()


def wide(value):
    return value.astype(F32)


def layer_kernel(
    tokens, gain, wq, wk, wv, wout, cot, gates,
    grad_out, layer_out, gate_out,
    rows_in, first_w, second_w, kv, relay, queries, top, low, acc, att, gated,
    grad, grad_in, line, line_in, out, out_core, out_in, gate_acc, gate_in, load, send, recv,
):
    ctx, head = lax.axis_index("ctx"), lax.axis_index("head")
    px, py = ctx // 4, ctx % 4
    pz, core = head // 2, head % 2

    def at_x(step):
        return ((px + step) % 4 * 4 + py, head)

    def at_y(step):
        return (px * 4 + (py + step) % 4, head)

    def at_z(step):
        return (ctx, (pz + step) % 4 * 2 + core)

    sibling = (ctx, pz * 2 + (1 - core))
    places = {"x": (px, at_x), "y": (py, at_y)}
    next_block = ((ctx + 1) % 16, head)
    two_on = ((px * 4 + (py + 1) % 4 + 2) % 16, head)
    back = (ctx + 14) % 16
    passer = (back // 4 * 4 + (back % 4 + 3) % 4, head)
    peers = [at(step) for at in (at_x, at_y) for step in (1, 2, 3)] + [at_z(1), at_z(3), sibling]
    peers += [((ctx + 15) % 16, head), passer]
    barrier = pltpu.get_barrier_semaphore()
    for peer in peers:
        pl.semaphore_signal(barrier, inc=1, device_id=peer, device_id_type=MESH)

    def fetch(number, source, target):
        copy = pltpu.make_async_copy(source, target, load.at[number])
        copy.start()
        return copy

    quarter = [pl.ds(128 * part, 128) for part in range(4)]
    token_loads = [fetch(part, tokens.at[rows], rows_in.at[rows]) for part, rows in enumerate(quarter)]
    key_load = fetch(4, wk, first_w.at[:, pl.ds(0, 256)])
    value_load = fetch(5, wv, first_w.at[:, pl.ds(256, 256)])
    query_load = fetch(6, wq, second_w)

    for part in range(4):
        token_loads[part].wait()

        def normalize(index, carry, part=part):
            rows = pl.ds(pl.multiple_of(part * 128 + index * 16, 16), 16)
            value = wide(rows_in[rows, :])
            moment = jnp.mean(value * value, axis=1, keepdims=True)
            rows_in[rows, :] = (value * lax.rsqrt(moment + EPSILON) * gain[...]).astype(BF16)
            return carry

        lax.fori_loop(0, 8, normalize, 0)

    links = Links(send, recv)
    key_load.wait()
    kv[0, 0] = jnp.dot(rows_in[...], first_w[:, 0:256], preferred_element_type=F32).astype(BF16)
    pl.semaphore_wait(barrier, len(peers))
    key_hop = links.start(kv.at[0, 0], kv.at[1, 0], next_block)
    value_load.wait()
    kv[0, 1] = jnp.dot(rows_in[...], first_w[:, 256:512], preferred_element_type=F32).astype(BF16)
    value_back = links.start(kv.at[0, 1], relay, at_y(3))
    value_hop = links.start(kv.at[0, 1], kv.at[1, 1], next_block)
    query_load.wait()
    queries[...] = jnp.dot(rows_in[...], second_w[...], preferred_element_type=F32).astype(BF16)

    strip = 768

    def cot_load(index):
        columns = pl.ds(pl.multiple_of(index * strip, 128), strip)
        return pltpu.make_async_copy(cot.at[:, columns], rows_in.at[:, columns], load.at[7 + index])

    def wout_load(index):
        columns = pl.ds(pl.multiple_of(index * strip, 128), strip)
        return pltpu.make_async_copy(wout.at[:, columns], rows_in.at[:, columns], load.at[14 + index])

    for index in range(7):
        cot_load(index).start()

    def attend(slot, pair):
        for half in range(2):
            rows = pl.ds(256 * half, 256)
            start, stop = (0, 256 * (half + 1)) if slot == 0 else (0, 512) if slot == 1 else (256 * half, 512)
            keys = kv[slot, 0, start:stop, 128 * pair : 128 * pair + 128]
            values = kv[slot, 1, start:stop, 128 * pair : 128 * pair + 128]
            for number in (2 * pair, 2 * pair + 1):
                here = pl.ds(128 * number, 128)
                scores = lax.dot_general(
                    queries[rows, here], keys, (((1,), (1,)), ((), ())), preferred_element_type=F32
                )
                if slot != 1:
                    row = lax.broadcasted_iota(jnp.int32, scores.shape, 0) + 256 * half
                    column = lax.broadcasted_iota(jnp.int32, scores.shape, 1) + start
                    allowed = column <= row if slot == 0 else column > row
                    scores = jnp.where(allowed, scores, -jnp.inf)
                peak = jnp.max(scores, axis=1, keepdims=True)
                if slot == 0:
                    lifted = jnp.exp2((scores - peak) * SCORE_POWER)
                    low[number, rows] = jnp.broadcast_to(jnp.sum(lifted, axis=1, keepdims=True), (256, 128))
                    acc[rows, here] = jnp.dot(lifted.astype(BF16), values, preferred_element_type=F32)
                    top[number, rows] = jnp.broadcast_to(peak, (256, 128))
                else:
                    before = top[number, rows]
                    peak = jnp.maximum(before, peak)
                    top[number, rows] = peak
                    fade = jnp.exp2((before - peak) * SCORE_POWER)
                    lifted = jnp.exp2((scores - peak[:, 0:1]) * SCORE_POWER)
                    low[number, rows] = low[number, rows] * fade + jnp.sum(lifted, axis=1, keepdims=True)
                    acc[rows, here] = acc[rows, here] * fade + jnp.dot(
                        lifted.astype(BF16), values, preferred_element_type=F32
                    )

    def close(pair):
        for number in (2 * pair, 2 * pair + 1):
            here = pl.ds(128 * number, 128)
            result = (acc[:, here] / low[number]).astype(BF16)
            att[:, here] = result
            gated[:, here] = (wide(result) * gates[:, here]).astype(BF16)

    attend(0, 0)
    attend(0, 1)
    key_hop.wait_recv()
    key_far = links.start(kv.at[1, 0], kv.at[2, 0], next_block)

    def turn_cot(index, carry):
        cot_load(index).wait()
        columns = pl.ds(pl.multiple_of(index * strip, 128), strip)
        second_w[columns, :] = rows_in[:, columns].T
        wout_load(index).start()
        return carry

    lax.fori_loop(0, 7, turn_cot, 0)
    value_back.wait_recv()
    value_far = links.start(relay, kv.at[2, 1], two_on)

    def turn_wout(index, carry):
        wout_load(index).wait()
        columns = pl.ds(pl.multiple_of(index * strip, 128), strip)
        first_w[columns, :] = rows_in[:, columns].T
        return carry

    lax.fori_loop(0, 7, turn_wout, 0)
    cot_t, wout_t = second_w, first_w

    def block_of(number, first, target, half):
        if first == "y":
            return grad.at[number, pl.ds(2 * half, 2), target]
        return grad.at[number, target, pl.ds(2 * half, 2)]

    firsts = ["y", "x", "y", "x"]
    gate_acc[...] = jnp.zeros_like(gate_acc)
    gate_in[0] = jnp.zeros((8, 128), F32)
    tall = 4 * GRAD_ROWS

    def grad_pair(pair):
        def chunk(index, carry):
            rows = pl.ds(pl.multiple_of(index * tall, 16), tall)
            product = jnp.dot(
                cot_t[rows, :], att[:, 256 * pair : 256 * pair + 256], preferred_element_type=F32
            )
            for side in range(2):
                number = 2 * pair + side
                mine = product[:, 128 * side : 128 * side + 128]
                grad[number, index] = mine.astype(BF16).reshape(4, GRAD_ROWS, 128)
                weighed = mine * wide(wout_t[rows, 128 * number : 128 * number + 128])
                gate_acc[number] += jnp.sum(weighed.reshape(tall // 8, 8, 128), axis=0)
            return carry

        lax.fori_loop(0, 4, chunk, 0)

    stage1 = {}

    def send_first(number):
        first = firsts[number]
        place, at = places[first]
        far, after, before = (place + 2) % 4, (place + 1) % 4, (place + 3) % 4
        box = grad_in.at[number]
        stage1[number] = [
            links.start(block_of(number, first, far, 0), box.at[0], at(1)),
            links.start(block_of(number, first, far, 1), box.at[1], at(3)),
            links.start(block_of(number, first, before, 0), box.at[2], at(3)),
            links.start(block_of(number, first, after, 1), box.at[3], at(1)),
        ]

    def relay_first(number):
        first = firsts[number]
        place, at = places[first]
        after, before = (place + 1) % 4, (place + 3) % 4
        box = grad_in.at[number]
        for slot, target, half, step in ((0, after, 0, 1), (1, before, 1, 3)):
            stage1[number][slot].wait_recv()
            box[slot] = (wide(box[slot]) + wide(block_of(number, first, target, half)[...])).astype(BF16)
            stage1[number].append(links.start(box.at[slot], box.at[4 + slot], at(step)))

    def end_first(number):
        first = firsts[number]
        place, _ = places[first]
        box = grad_in.at[number]
        for half in range(2):
            stage1[number][2 + half].wait_recv()
            stage1[number][4 + half].wait_recv()
            total = wide(block_of(number, first, place, half)[...]) + wide(box[2 + half]) + wide(box[4 + half])
            line[number, pl.ds(2 * half, 2)] = total.astype(BF16)

    stage2 = {}
    cuts = (pl.ds(0, SPLIT), pl.ds(SPLIT, GRAD_ROWS - SPLIT))
    sizes = (pl.ds(0, SPLIT), pl.ds(0, GRAD_ROWS - SPLIT))

    def send_second(number):
        place, at = places["x" if firsts[number] == "y" else "y"]
        far, after, before = (place + 2) % 4, (place + 1) % 4, (place + 3) % 4
        mine, box = line.at[number], line_in.at[number]
        stage2[number] = [
            links.start(mine.at[far, cuts[0]], box.at[0, sizes[0]], at(1)),
            links.start(mine.at[far, cuts[1]], box.at[1, sizes[1]], at(3)),
            links.start(mine.at[before, cuts[0]], box.at[2, sizes[0]], at(3)),
            links.start(mine.at[after, cuts[1]], box.at[3, sizes[1]], at(1)),
        ]

    def relay_second(number):
        place, at = places["x" if firsts[number] == "y" else "y"]
        after, before = (place + 1) % 4, (place + 3) % 4
        mine, box = line.at[number], line_in.at[number]
        for slot, target, step in ((0, after, 1), (1, before, 3)):
            stage2[number][slot].wait_recv()
            part = box.at[slot, sizes[slot]]
            part[...] = (wide(part[...]) + wide(mine[target, cuts[slot]])).astype(BF16)
            stage2[number].append(links.start(part, box.at[4 + slot, sizes[slot]], at(step)))

    def end_second(number):
        place, _ = places["x" if firsts[number] == "y" else "y"]
        mine, box = line.at[number], line_in.at[number]
        for half in range(2):
            stage2[number][2 + half].wait_recv()
            stage2[number][4 + half].wait_recv()
            grad_out[number, cuts[half]] = (
                wide(mine[place, cuts[half]])
                + wide(box[2 + half, sizes[half]])
                + wide(box[4 + half, sizes[half]])
            )

    across = []

    def out_part(place):
        rows = pl.ds(pl.multiple_of(place * (2 * OUT_ROWS), 16), 2 * OUT_ROWS)
        product = lax.dot_general(
            wout_t[rows, :], gated[...], (((1,), (1,)), ((), ())), preferred_element_type=F32
        ).astype(BF16)
        out[place] = product.reshape(2, OUT_ROWS, 512)
        across.append(links.start(out.at[place, 1 - core], out_core.at[place], sibling))

    key_hop_done = value_hop
    key_hop_done.wait_recv()

    @pl.when(ctx >= 1)
    def _():
        attend(1, 0)
        attend(1, 1)

    key_far.wait_recv()
    value_far.wait_recv()

    @pl.when(ctx >= 2)
    def _():
        attend(2, 0)

    close(0)
    grad_pair(0)
    send_first(0)
    send_first(1)

    @pl.when(ctx >= 2)
    def _():
        attend(2, 1)

    close(1)
    order = [(pz + step) % 4 for step in (2, 1, 3, 0)]
    for place in order:
        out_part(place)
    relay_first(0)
    relay_first(1)
    grad_pair(1)
    send_first(2)
    send_first(3)

    for number in range(4):
        gate_in[0, pl.ds(number, 1)] = jnp.sum(gate_acc[number], axis=0, keepdims=True)
    gate_y = [links.start(gate_in.at[0], gate_in.at[step], at_y(step)) for step in (1, 2, 3)]

    def add_core(index):
        across[index].wait_recv()
        place = order[index]

        def piece(step, carry):
            rows = pl.ds(pl.multiple_of(step * 112, 16), 112)
            out_core[place, rows] = (wide(out[place, core, rows]) + wide(out_core[place, rows])).astype(BF16)
            return carry

        lax.fori_loop(0, OUT_ROWS // 112, piece, 0)

    far, after, before = order[0], order[1], order[2]
    upper, lower = pl.ds(0, HALF_OUT), pl.ds(HALF_OUT, HALF_OUT)
    add_core(0)
    ring = [
        links.start(out_core.at[far, upper], out_in.at[0], at_z(1)),
        links.start(out_core.at[far, lower], out_in.at[1], at_z(3)),
    ]
    add_core(1)
    add_core(2)
    ring += [
        links.start(out_core.at[before, upper], out_in.at[2], at_z(3)),
        links.start(out_core.at[after, lower], out_in.at[3], at_z(1)),
    ]
    for number in (0, 1):
        end_first(number)
        send_second(number)
    add_core(3)
    relay_first(2)
    relay_first(3)
    for slot, target, rows, step in ((0, after, 0, 1), (1, before, HALF_OUT, 3)):
        ring[slot].wait_recv()

        def piece(index, carry, slot=slot, target=target, rows=rows):
            here = pl.ds(pl.multiple_of(index * 112, 16), 112)
            there = pl.ds(pl.multiple_of(index * 112 + rows, 16), 112)
            out_in[slot, here] = (wide(out_in[slot, here]) + wide(out_core[target, there])).astype(BF16)
            return carry

        lax.fori_loop(0, HALF_OUT // 112, piece, 0)
        ring.append(links.start(out_in.at[slot], out_in.at[4 + slot], at_z(step)))

    relay_second(0)
    relay_second(1)
    for copy in gate_y:
        copy.wait_recv()
    gate_in[4] = gate_in[0] + gate_in[1] + gate_in[2] + gate_in[3]
    gate_x = [links.start(gate_in.at[4], gate_in.at[4 + step], at_x(step)) for step in (1, 2, 3)]
    for number in (2, 3):
        end_first(number)
        send_second(number)
    end_second(0)
    end_second(1)
    for copy in gate_x:
        copy.wait_recv()
    gate_out[...] = gate_in[4] + gate_in[5] + gate_in[6] + gate_in[7]
    relay_second(2)
    relay_second(3)
    for half in range(2):
        ring[2 + half].wait_recv()
        ring[4 + half].wait_recv()

        def piece(index, carry, half=half):
            here = pl.ds(pl.multiple_of(index * 112, 16), 112)
            there = pl.ds(pl.multiple_of(index * 112 + half * HALF_OUT, 16), 112)
            total = wide(out_core[pz, there]) + wide(out_in[2 + half, here]) + wide(out_in[4 + half, here])
            layer_out[there, :] = total.astype(BF16)
            return carry

        lax.fori_loop(0, HALF_OUT // 112, piece, 0)
    end_second(2)
    end_second(3)
    links.finish()


def run_layer(tokens, gain, wq, wk, wv, wout, cot, gates):
    vmem = pl.BlockSpec(memory_space=pltpu.VMEM)
    hbm = pl.BlockSpec(memory_space=pl.ANY)
    wide_w = pltpu.VMEM((5376, 512), BF16)
    return pl.pallas_call(
        layer_kernel,
        out_shape=(
            jax.ShapeDtypeStruct((4, GRAD_ROWS, 128), F32),
            jax.ShapeDtypeStruct((OUT_ROWS, 512), BF16),
            jax.ShapeDtypeStruct((8, 128), F32),
        ),
        in_specs=[hbm, vmem, hbm, hbm, hbm, hbm, hbm, vmem],
        out_specs=(vmem,) * 3,
        scratch_shapes=[
            pltpu.VMEM((512, 5376), BF16),
            wide_w,
            wide_w,
            pltpu.VMEM((3, 2, 512, 256), BF16),
            pltpu.VMEM((512, 256), BF16),
            pltpu.VMEM((512, 512), BF16),
            pltpu.VMEM((4, 512, 128), F32),
            pltpu.VMEM((4, 512, 128), F32),
            pltpu.VMEM((512, 512), F32),
            pltpu.VMEM((512, 512), BF16),
            pltpu.VMEM((512, 512), BF16),
            pltpu.VMEM((4, 4, 4, GRAD_ROWS, 128), BF16),
            pltpu.VMEM((4, 6, 2, GRAD_ROWS, 128), BF16),
            pltpu.VMEM((4, 4, GRAD_ROWS, 128), BF16),
            pltpu.VMEM((4, 6, SPLIT, 128), BF16),
            pltpu.VMEM((4, 2, OUT_ROWS, 512), BF16),
            pltpu.VMEM((4, OUT_ROWS, 512), BF16),
            pltpu.VMEM((6, HALF_OUT, 512), BF16),
            pltpu.VMEM((4, 8, 128), F32),
            pltpu.VMEM((8, 8, 128), F32),
            pltpu.SemaphoreType.DMA((21,)),
            pltpu.SemaphoreType.DMA((69,)),
            pltpu.SemaphoreType.DMA((69,)),
        ],
        compiler_params=pltpu.CompilerParams(
            collective_id=0, has_side_effects=True, vmem_limit_bytes=58 * 2**20
        ),
    )(tokens, gain, wq, wk, wv, wout, cot, gates)


def hard_concrete(mask_logit, noise_draw):
    stretched = jax.nn.sigmoid(
        (jnp.log(noise_draw) - jnp.log(1.0 - noise_draw) + mask_logit) / BETA
    )
    shifted = stretched * (ZETA - GAMMA) + GAMMA
    gate_value = jnp.clip(shifted, 0.0, 1.0)
    inside = jnp.logical_and(shifted > 0.0, shifted < 1.0)
    gate_slope = jnp.where(inside, (ZETA - GAMMA) * stretched * (1.0 - stretched) / BETA, 0.0)
    expected = jax.nn.sigmoid(mask_logit - BETA * math.log(-GAMMA / ZETA))
    return (gate_value, gate_slope, PENALTY * expected * (1.0 - expected))


def body(tokens, norm_gain, w_query, w_key, value_weight, w_out, mask_logit, noise_draw, cotangent):
    local_heads = mask_logit.shape[0]
    inv_root = 1.0 / math.sqrt(tokens.shape[0] * lax.axis_size("ctx"))
    gate_value, gate_slope, penalty_term = hard_concrete(mask_logit, noise_draw)
    gate_columns = jnp.repeat(gate_value, HEAD_SIZE)
    grad_t, out_t, gate_rows = run_layer(
        tokens, norm_gain.astype(F32)[None, :], w_query, w_key, value_weight, w_out, cotangent, gate_columns[None, :]
    )
    layer_out = out_t.T
    summed = jnp.moveaxis(grad_t, 1, 2).reshape(local_heads * HEAD_SIZE, grad_t.shape[1])
    grad_out_proj = summed * gate_columns[:, None] * inv_root
    gate_product = jnp.sum(gate_rows[:local_heads], axis=1)
    grad_logit = gate_product * inv_root * gate_slope + penalty_term
    return (layer_out, grad_logit, grad_out_proj)


def solution(mesh):
    return jax.shard_map(
        body,
        mesh=mesh,
        in_specs=(
            P("ctx", None),
            P(),
            P(None, "head"),
            P(None, "head"),
            P(None, "head"),
            P("head", None),
            P("head"),
            P("head"),
            P("ctx", None),
        ),
        out_specs=(P("ctx", "head"), P("head"), P("head", "ctx")),
        check_vma=False,
    )
```

time: 143 us -> 82.2 us (0.57)
  matrix products: 30 us -> 0 us
  local copies, waits for them, and re-layouts: 23 us -> 4.05 us
  starting transfers between devices: 17.3 us -> 0 us
  Pallas kernels: 57.7 us -> 73.1 us
  other arithmetic: 13.6 us -> 4.06 us
    dot_general x4 -> x0, matrix products: 18.7 us -> none  [the longest x1 8.16 us: body(): jnp.dot(normed, w_query, preferred_element_type=jnp.float32)]
    unnamed x21 -> x3, local copies, waits for them, and re-layouts: 19.3 us -> 1.99 us
    ppermute x4 -> x0, starting transfers between devices: 17.3 us -> none  [shifted_2(): lax.ppermute(value, axis, [(source, source + steps) for source in range(f...]
    pallas_call x1, Pallas kernels: 57.7 us -> 73.1 us  [run_layer(): pl.pallas_call(layer_kernel, out_shape=(jax.ShapeDtypeStruct((4, GRAD_ROW...]
    sub x1 -> x0, matrix products: 11.3 us -> none  [body(): lifted = jnp.exp(scores - row_max)]
    reduce_sum x1 -> x0, other arithmetic: 4.14 us -> none  [body(): moment = jnp.mean(jnp.square(widened), axis=1, keepdims=True)]
    reshape x3 -> x0, local copies, waits for them, and re-layouts: 3.56 us -> none  [the longest x1 1.25 us: body(): attended.astype(jnp.bfloat16).reshape(tok_rows, local_heads * HEAD_SIZE)]
    concatenate x2 -> x0, other arithmetic: 2.32 us -> none  [the longest x1 1.16 us: body(): jnp.concatenate([pair[1] for pair in earlier] + [rows_of_values], axis=0)]
  transfers between devices with their start and end apart: 4 -> 0, of which waited for: 0 -> 0; matrix products, arithmetic and copies ran while one was open for 22% -> 0% of each run, Pallas kernels for 0% -> 0%
where the time goes in v2:
time: 82.2 us; the launch traced here: 81.9 us
  Pallas kernels  73.1 us (89%)
  other arithmetic  4.06 us (5%)
  local copies, waits for them, and re-layouts  4.05 us (5%)
    pallas_call x1, Pallas kernels, run_layer(): pl.pallas_call(layer_kernel, out_shape=(jax.ShapeDtypeStruct((4, GRAD_ROW...  73.1 us
    mul x1, other arithmetic, body(): grad_out_proj = summed * gate_columns[:, None] * inv_root  2.04 us
    unnamed x3, local copies, waits for them, and re-layouts  1.99 us

profile of v2, /device:TPU:0, one launch (start us, length us, event | category | flops | bytes accessed | tf_op | source)
XLA Modules:
  0.0 81.9 jit_solution(13305500135916803742)
XLA Ops:
  0.6 1.3 %reshape.11.gain = f32[1,5376]{1,0:T(1,128)} reshape(bf16[5376]{0:T(1024)(128)(2,1)} %param.10) | data formatting | bytes 32256 | tf_op jit(solution)/shard_map/broadcast_in_dim | solution.py:483
  2.0 0.7 add_clamp_fusion
  2.6 0.7 broadcast_in_dim.12
  3.3 0.0 copy-start
  3.3 73.1 %shard_map.112 = (f32[4,336,128]{2,1,0:T(8,128)}, bf16[672,512]{1,0:T(8,128)(2,1)}, f32[8,128]{1,0:T(8,128)}) custom-call(bf16[512,5376]{1,0:T(8,128)(2,1)} %tokens.1, f32[1,5376]{1,0:T(1,128)} %reshape.11.gain, bf16[5376,512]{1,0:T(8,128)(2,1)} %wq.1, bf16[5376,256]{1,0:T(8,128)(2,1)} %wk.1, bf16[5376,256]{1,0:T(8,128)(2,1)} %wv.1, bf16[512,5376]{1,0:T(8,128)(2,1)} %wout.1, ...), custom_call_target="tpu_custom_call" | custom-call | tf_op jit(solution)/shard_map/pallas_call | solution.py:425
  76.4 0.8 slice_reduce_fusion
  77.2 0.0 copy-done
  77.2 0.5 multiply_add_fusion
  77.8 0.1 broadcast_bitcast_fusion
  77.8 2.0 %fusion = f32[512,336]{0,1:T(8,128)} fusion(f32[512]{0:T(512)S(1)} %broadcast_bitcast_fusion, f32[4,336,128]{2,1,0:T(8,128)} %get-tuple-element.8), kind=kLoop, calls=%fused_computation.1 | loop fusion | flops 344064 | bytes 1378304 | tf_op jit(solution)/shard_map/mul | solution.py:487
  79.9 2.0 %copy.16 = bf16[512,672]{0,1:T(8,128)(2,1)} copy(bf16[512,672]{0,1:T(8,128)(2,1)} %bitcast.12) | data formatting | bytes 1376256
Async XLA Ops:
  3.3 73.9 %copy-start = (f32[4]{0:T(128)S(1)}, f32[4]{0:T(128)}, u32[]{:S(2)}) copy-start(f32[4]{0:T(128)} %param.15) | copy-start | bytes 52

commit v3 on v2

--- a/solution.py
+++ b/solution.py
@@ -25,6 +25,19 @@
 OUT_ROWS = 672
 HALF_OUT = 336
 SPLIT = 176
+INV_ROOT = 1.0 / math.sqrt(8192)
+
+
+def hard_concrete(mask_logit, noise_draw):
+    stretched = jax.nn.sigmoid(
+        (jnp.log(noise_draw) - jnp.log(1.0 - noise_draw) + mask_logit) / BETA
+    )
+    shifted = stretched * (ZETA - GAMMA) + GAMMA
+    gate_value = jnp.clip(shifted, 0.0, 1.0)
+    inside = jnp.logical_and(shifted > 0.0, shifted < 1.0)
+    gate_slope = jnp.where(inside, (ZETA - GAMMA) * stretched * (1.0 - stretched) / BETA, 0.0)
+    expected = jax.nn.sigmoid(mask_logit - BETA * math.log(-GAMMA / ZETA))
+    return (gate_value, gate_slope, PENALTY * expected * (1.0 - expected))
 
 
 class Links:
@@ -55,9 +68,9 @@
 
 
 def layer_kernel(
-    tokens, gain, wq, wk, wv, wout, cot, gates,
-    grad_out, layer_out, gate_out,
-    rows_in, first_w, second_w, kv, relay, queries, top, low, acc, att, gated,
+    tokens, gain, wq, wk, wv, wout, mask_logit, noise_draw, cot,
+    layer_out, gate_out, grad_out,
+    rows_in, cot_in, first_w, second_w, scale, keys_at, values_at, relay_k, relay_v, queries, top, low, acc, att, gated,
     grad, grad_in, line, line_in, out, out_core, out_in, gate_acc, gate_in, load, send, recv,
 ):
     ctx, head = lax.axis_index("ctx"), lax.axis_index("head")
@@ -92,102 +105,145 @@
 
     quarter = [pl.ds(128 * part, 128) for part in range(4)]
     token_loads = [fetch(part, tokens.at[rows], rows_in.at[rows]) for part, rows in enumerate(quarter)]
-    key_load = fetch(4, wk, first_w.at[:, pl.ds(0, 256)])
-    value_load = fetch(5, wv, first_w.at[:, pl.ds(256, 256)])
-    query_load = fetch(6, wq, second_w)
+    weight_loads = []
+    weight_copies = [
+        (4, wk.at[:, pl.ds(0, 128)], first_w.at[:, pl.ds(0, 128)]),
+        (5, wv.at[:, pl.ds(0, 128)], first_w.at[:, pl.ds(128, 128)]),
+        (6, wk.at[:, pl.ds(128, 128)], first_w.at[:, pl.ds(256, 128)]),
+        (7, wv.at[:, pl.ds(128, 128)], first_w.at[:, pl.ds(384, 128)]),
+        (8, wq, second_w),
+    ]
+
+    strip = 768
+
+    def cot_load(index):
+        columns = pl.ds(pl.multiple_of(index * strip, 128), strip)
+        return pltpu.make_async_copy(cot.at[:, columns], cot_in.at[:, columns], load.at[9 + index])
+
+    def wout_load(index):
+        columns = pl.ds(pl.multiple_of(index * strip, 128), strip)
+        return pltpu.make_async_copy(wout.at[:, columns], rows_in.at[:, columns], load.at[16 + index])
 
     for part in range(4):
         token_loads[part].wait()
-
-        def normalize(index, carry, part=part):
-            rows = pl.ds(pl.multiple_of(part * 128 + index * 16, 16), 16)
-            value = wide(rows_in[rows, :])
-            moment = jnp.mean(value * value, axis=1, keepdims=True)
-            rows_in[rows, :] = (value * lax.rsqrt(moment + EPSILON) * gain[...]).astype(BF16)
+        for copy in weight_copies[0:2] if part == 0 else weight_copies[2:4] if part == 2 else weight_copies[4:] if part == 3 else []:
+            weight_loads.append(fetch(*copy))
+
+        def weigh(index, carry, part=part):
+            rows = pl.ds(pl.multiple_of(part * 128 + index * 32, 32), 32)
+            total = jnp.zeros((32, 128), F32)
+            for tile in range(42):
+                columns = slice(128 * tile, 128 * tile + 128)
+                value = rows_in[rows, columns]
+                total += wide(value) * wide(value)
+                rows_in[rows, columns] = value * gain[columns][None, :]
+            scale[rows, :] = total
             return carry
 
-        lax.fori_loop(0, 8, normalize, 0)
-
-    links = Links(send, recv)
-    key_load.wait()
-    kv[0, 0] = jnp.dot(rows_in[...], first_w[:, 0:256], preferred_element_type=F32).astype(BF16)
-    pl.semaphore_wait(barrier, len(peers))
-    key_hop = links.start(kv.at[0, 0], kv.at[1, 0], next_block)
-    value_load.wait()
-    kv[0, 1] = jnp.dot(rows_in[...], first_w[:, 256:512], preferred_element_type=F32).astype(BF16)
-    value_back = links.start(kv.at[0, 1], relay, at_y(3))
-    value_hop = links.start(kv.at[0, 1], kv.at[1, 1], next_block)
-    query_load.wait()
-    queries[...] = jnp.dot(rows_in[...], second_w[...], preferred_element_type=F32).astype(BF16)
-
-    strip = 768
-
-    def cot_load(index):
-        columns = pl.ds(pl.multiple_of(index * strip, 128), strip)
-        return pltpu.make_async_copy(cot.at[:, columns], rows_in.at[:, columns], load.at[7 + index])
-
-    def wout_load(index):
-        columns = pl.ds(pl.multiple_of(index * strip, 128), strip)
-        return pltpu.make_async_copy(wout.at[:, columns], rows_in.at[:, columns], load.at[14 + index])
+        lax.fori_loop(0, 4, weigh, 0)
 
     for index in range(7):
         cot_load(index).start()
+    moment = jnp.sum(scale[...], axis=1, keepdims=True) * (1.0 / 5376)
+    scale[...] = jnp.broadcast_to(lax.rsqrt(moment + EPSILON), (512, 128))
+
+    def project(weight):
+        product = jnp.dot(rows_in[...], weight, preferred_element_type=F32)
+        return (product * jnp.concatenate([scale[...]] * (weight.shape[1] // 128), axis=1)).astype(BF16)
+
+    links = Links(send, recv)
+
+    def keys_and_values(pair):
+        for copy in weight_loads[2 * pair : 2 * pair + 2]:
+            copy.wait()
+        both = project(first_w[:, 256 * pair : 256 * pair + 256])
+        keys_at[0, pair] = both[:, 0:128]
+        values_at[0, pair] = both[:, 128:256].T
+
+    def pass_on(sources, targets, device):
+        return [links.start(source, target, device) for source, target in zip(sources, targets)]
+
+    def arrive(copies):
+        for copy in copies:
+            copy.wait_recv()
+
+    def held(slot, pair):
+        return keys_at.at[slot, pair], values_at.at[slot, pair]
+
+    keys_and_values(0)
+    pl.semaphore_wait(barrier, len(peers))
+    hop0 = pass_on(held(0, 0), held(1, 0), next_block)
+    keys_and_values(1)
+    back1 = pass_on(held(0, 1), (relay_k, relay_v), at_y(3))
+    hop1 = pass_on(held(0, 1), held(1, 1), next_block)
+    weight_loads[4].wait()
+    queries[...] = project(second_w[...])
+
+    for index in range(7):
+        wout_load(index).start()
 
     def attend(slot, pair):
-        for half in range(2):
-            rows = pl.ds(256 * half, 256)
-            start, stop = (0, 256 * (half + 1)) if slot == 0 else (0, 512) if slot == 1 else (256 * half, 512)
-            keys = kv[slot, 0, start:stop, 128 * pair : 128 * pair + 128]
-            values = kv[slot, 1, start:stop, 128 * pair : 128 * pair + 128]
+        for block in range(4):
+            rows = pl.ds(128 * block, 128)
+            start, stop = (0, 128 * (block + 1)) if slot == 0 else (0, 512) if slot == 1 else (128 * block, 512)
+            keys = keys_at[slot, pair, start:stop, :]
+            values = values_at[slot, pair, :, start:stop]
             for number in (2 * pair, 2 * pair + 1):
-                here = pl.ds(128 * number, 128)
+                here, one = pl.ds(128 * number, 128), pl.ds(number, 1)
                 scores = lax.dot_general(
-                    queries[rows, here], keys, (((1,), (1,)), ((), ())), preferred_element_type=F32
+                    keys, queries[rows, here], (((1,), (1,)), ((), ())), preferred_element_type=F32
                 )
                 if slot != 1:
-                    row = lax.broadcasted_iota(jnp.int32, scores.shape, 0) + 256 * half
-                    column = lax.broadcasted_iota(jnp.int32, scores.shape, 1) + start
-                    allowed = column <= row if slot == 0 else column > row
-                    scores = jnp.where(allowed, scores, -jnp.inf)
-                peak = jnp.max(scores, axis=1, keepdims=True)
-                if slot == 0:
-                    lifted = jnp.exp2((scores - peak) * SCORE_POWER)
-                    low[number, rows] = jnp.broadcast_to(jnp.sum(lifted, axis=1, keepdims=True), (256, 128))
-                    acc[rows, here] = jnp.dot(lifted.astype(BF16), values, preferred_element_type=F32)
-                    top[number, rows] = jnp.broadcast_to(peak, (256, 128))
+                    key = lax.broadcasted_iota(jnp.int32, scores.shape, 0) + start
+                    query = lax.broadcasted_iota(jnp.int32, scores.shape, 1) + 128 * block
+                    scores = jnp.where(key <= query if slot == 0 else key > query, scores, -jnp.inf)
+                peak = jnp.max(scores, axis=0, keepdims=True)
+                if slot > 0:
+                    before = top[one, rows]
+                    peak = jnp.maximum(before, peak)
+                    fade = jnp.exp2((before - peak) * SCORE_POWER)
+                lifted = jnp.exp2((scores - peak) * SCORE_POWER)
+                total = jnp.sum(lifted, axis=0, keepdims=True)
+                mixed = jnp.dot(values, lifted.astype(BF16), preferred_element_type=F32)
+                top[one, rows] = peak
+                if slot > 0:
+                    low[one, rows] = low[one, rows] * fade + total
+                    acc[here, rows] = acc[here, rows] * fade + mixed
                 else:
-                    before = top[number, rows]
-                    peak = jnp.maximum(before, peak)
-                    top[number, rows] = peak
-                    fade = jnp.exp2((before - peak) * SCORE_POWER)
-                    lifted = jnp.exp2((scores - peak[:, 0:1]) * SCORE_POWER)
-                    low[number, rows] = low[number, rows] * fade + jnp.sum(lifted, axis=1, keepdims=True)
-                    acc[rows, here] = acc[rows, here] * fade + jnp.dot(
-                        lifted.astype(BF16), values, preferred_element_type=F32
-                    )
+                    low[one, rows] = total
+                    acc[here, rows] = mixed
 
     def close(pair):
         for number in (2 * pair, 2 * pair + 1):
             here = pl.ds(128 * number, 128)
-            result = (acc[:, here] / low[number]).astype(BF16)
-            att[:, here] = result
-            gated[:, here] = (wide(result) * gates[:, here]).astype(BF16)
-
+            result = (acc[here, :] * (1.0 / low[pl.ds(number, 1), :])).astype(BF16)
+            att[here, :] = result
+            gated[here, :] = (wide(result) * gates[number][0:1, 0:1]).astype(BF16)
+
+    gates, slopes, penalties = zip(
+        *(
+            hard_concrete(jnp.full((8, 128), mask_logit[number], F32), jnp.full((8, 128), noise_draw[number], F32))
+            for number in range(4)
+        )
+    )
     attend(0, 0)
     attend(0, 1)
-    key_hop.wait_recv()
-    key_far = links.start(kv.at[1, 0], kv.at[2, 0], next_block)
+    arrive(hop0)
+    far0 = pass_on(held(1, 0), held(2, 0), next_block)
 
     def turn_cot(index, carry):
         cot_load(index).wait()
         columns = pl.ds(pl.multiple_of(index * strip, 128), strip)
-        second_w[columns, :] = rows_in[:, columns].T
-        wout_load(index).start()
+        second_w[columns, :] = cot_in[:, columns].T
         return carry
 
     lax.fori_loop(0, 7, turn_cot, 0)
-    value_back.wait_recv()
-    value_far = links.start(relay, kv.at[2, 1], two_on)
+    arrive(back1)
+    far1 = pass_on((relay_k, relay_v), held(2, 1), two_on)
+
+    @pl.when(ctx >= 1)
+    def _():
+        attend(1, 0)
 
     def turn_wout(index, carry):
         wout_load(index).wait()
@@ -211,8 +267,9 @@
     def grad_pair(pair):
         def chunk(index, carry):
             rows = pl.ds(pl.multiple_of(index * tall, 16), tall)
-            product = jnp.dot(
-                cot_t[rows, :], att[:, 256 * pair : 256 * pair + 256], preferred_element_type=F32
+            product = lax.dot_general(
+                cot_t[rows, :], att[256 * pair : 256 * pair + 256, :], (((1,), (1,)), ((), ())),
+                preferred_element_type=F32,
             )
             for side in range(2):
                 number = 2 * pair + side
@@ -289,32 +346,22 @@
         for half in range(2):
             stage2[number][2 + half].wait_recv()
             stage2[number][4 + half].wait_recv()
-            grad_out[number, cuts[half]] = (
+            total = (
                 wide(mine[place, cuts[half]])
                 + wide(box[2 + half, sizes[half]])
                 + wide(box[4 + half, sizes[half]])
             )
+            grad_out[cuts[half], 128 * number : 128 * number + 128] = total * (gates[number][0:1, 0:1] * INV_ROOT)
 
     across = []
 
     def out_part(place):
         rows = pl.ds(pl.multiple_of(place * (2 * OUT_ROWS), 16), 2 * OUT_ROWS)
-        product = lax.dot_general(
-            wout_t[rows, :], gated[...], (((1,), (1,)), ((), ())), preferred_element_type=F32
-        ).astype(BF16)
+        product = jnp.dot(wout_t[rows, :], gated[...], preferred_element_type=F32).astype(BF16)
         out[place] = product.reshape(2, OUT_ROWS, 512)
         across.append(links.start(out.at[place, 1 - core], out_core.at[place], sibling))
 
-    key_hop_done = value_hop
-    key_hop_done.wait_recv()
-
-    @pl.when(ctx >= 1)
-    def _():
-        attend(1, 0)
-        attend(1, 1)
-
-    key_far.wait_recv()
-    value_far.wait_recv()
+    arrive(far0)
 
     @pl.when(ctx >= 2)
     def _():
@@ -324,6 +371,13 @@
     grad_pair(0)
     send_first(0)
     send_first(1)
+    arrive(hop1)
+
+    @pl.when(ctx >= 1)
+    def _():
+        attend(1, 1)
+
+    arrive(far1)
 
     @pl.when(ctx >= 2)
     def _():
@@ -331,17 +385,8 @@
 
     close(1)
     order = [(pz + step) % 4 for step in (2, 1, 3, 0)]
-    for place in order:
+    for place in order[:3]:
         out_part(place)
-    relay_first(0)
-    relay_first(1)
-    grad_pair(1)
-    send_first(2)
-    send_first(3)
-
-    for number in range(4):
-        gate_in[0, pl.ds(number, 1)] = jnp.sum(gate_acc[number], axis=0, keepdims=True)
-    gate_y = [links.start(gate_in.at[0], gate_in.at[step], at_y(step)) for step in (1, 2, 3)]
 
     def add_core(index):
         across[index].wait_recv()
@@ -361,16 +406,27 @@
         links.start(out_core.at[far, upper], out_in.at[0], at_z(1)),
         links.start(out_core.at[far, lower], out_in.at[1], at_z(3)),
     ]
+    relay_first(0)
+    relay_first(1)
+    grad_pair(1)
+    send_first(2)
+    send_first(3)
     add_core(1)
     add_core(2)
     ring += [
         links.start(out_core.at[before, upper], out_in.at[2], at_z(3)),
         links.start(out_core.at[after, lower], out_in.at[3], at_z(1)),
     ]
+
+    out_part(order[3])
+
+    for number in range(4):
+        gate_in[0, pl.ds(number, 1)] = jnp.sum(gate_acc[number], axis=0, keepdims=True)
+    gate_y = [links.start(gate_in.at[0], gate_in.at[step], at_y(step)) for step in (1, 2, 3)]
+    add_core(3)
     for number in (0, 1):
         end_first(number)
         send_second(number)
-    add_core(3)
     relay_first(2)
     relay_first(3)
     for slot, target, rows, step in ((0, after, 0, 1), (1, before, HALF_OUT, 3)):
@@ -385,12 +441,12 @@
         lax.fori_loop(0, HALF_OUT // 112, piece, 0)
         ring.append(links.start(out_in.at[slot], out_in.at[4 + slot], at_z(step)))
 
-    relay_second(0)
-    relay_second(1)
     for copy in gate_y:
         copy.wait_recv()
     gate_in[4] = gate_in[0] + gate_in[1] + gate_in[2] + gate_in[3]
     gate_x = [links.start(gate_in.at[4], gate_in.at[4 + step], at_x(step)) for step in (1, 2, 3)]
+    relay_second(0)
+    relay_second(1)
     for number in (2, 3):
         end_first(number)
         send_second(number)
@@ -398,7 +454,11 @@
     end_second(1)
     for copy in gate_x:
         copy.wait_recv()
-    gate_out[...] = gate_in[4] + gate_in[5] + gate_in[6] + gate_in[7]
+    gate_sum = gate_in[4] + gate_in[5] + gate_in[6] + gate_in[7]
+    for number in range(4):
+        product = jnp.sum(gate_sum[number : number + 1, :], axis=1, keepdims=True)
+        answer = product * INV_ROOT * slopes[number] + penalties[number]
+        gate_out[pl.ds(number, 1), :] = jnp.broadcast_to(answer[0:1, :], (1, 128))
     relay_second(2)
     relay_second(3)
     for half in range(2):
@@ -418,28 +478,39 @@
     links.finish()
 
 
-def run_layer(tokens, gain, wq, wk, wv, wout, cot, gates):
+def deliver_kernel(layer_in, gate_in, grad_in, layer_out, gate_out, grad_out):
+    layer_out[...] = layer_in[...]
+    grad_out[...] = grad_in[...]
+    for number in range(4):
+        gate_out[number] = gate_in[number, 0]
+
+
+def body(*args):
     vmem = pl.BlockSpec(memory_space=pltpu.VMEM)
+    smem = pl.BlockSpec(memory_space=pltpu.SMEM)
     hbm = pl.BlockSpec(memory_space=pl.ANY)
     wide_w = pltpu.VMEM((5376, 512), BF16)
-    return pl.pallas_call(
+    tokens, norm_gain, *rest = args
+    layer_shape = jax.ShapeDtypeStruct((OUT_ROWS, 512), BF16)
+    grad_shape = jax.ShapeDtypeStruct((GRAD_ROWS, 512), F32)
+    results = pl.pallas_call(
         layer_kernel,
-        out_shape=(
-            jax.ShapeDtypeStruct((4, GRAD_ROWS, 128), F32),
-            jax.ShapeDtypeStruct((OUT_ROWS, 512), BF16),
-            jax.ShapeDtypeStruct((8, 128), F32),
-        ),
-        in_specs=[hbm, vmem, hbm, hbm, hbm, hbm, hbm, vmem],
+        out_shape=(layer_shape, jax.ShapeDtypeStruct((8, 128), F32), grad_shape),
+        in_specs=[hbm, vmem, hbm, hbm, hbm, hbm, smem, smem, hbm],
         out_specs=(vmem,) * 3,
         scratch_shapes=[
             pltpu.VMEM((512, 5376), BF16),
+            pltpu.VMEM((512, 5376), BF16),
             wide_w,
             wide_w,
-            pltpu.VMEM((3, 2, 512, 256), BF16),
-            pltpu.VMEM((512, 256), BF16),
+            pltpu.VMEM((512, 128), F32),
+            pltpu.VMEM((3, 2, 512, 128), BF16),
+            pltpu.VMEM((3, 2, 128, 512), BF16),
+            pltpu.VMEM((512, 128), BF16),
+            pltpu.VMEM((128, 512), BF16),
             pltpu.VMEM((512, 512), BF16),
-            pltpu.VMEM((4, 512, 128), F32),
-            pltpu.VMEM((4, 512, 128), F32),
+            pltpu.VMEM((8, 512), F32),
+            pltpu.VMEM((8, 512), F32),
             pltpu.VMEM((512, 512), F32),
             pltpu.VMEM((512, 512), BF16),
             pltpu.VMEM((512, 512), BF16),
@@ -452,42 +523,21 @@
             pltpu.VMEM((6, HALF_OUT, 512), BF16),
             pltpu.VMEM((4, 8, 128), F32),
             pltpu.VMEM((8, 8, 128), F32),
-            pltpu.SemaphoreType.DMA((21,)),
-            pltpu.SemaphoreType.DMA((69,)),
-            pltpu.SemaphoreType.DMA((69,)),
+            pltpu.SemaphoreType.DMA((23,)),
+            pltpu.SemaphoreType.DMA((74,)),
+            pltpu.SemaphoreType.DMA((74,)),
         ],
         compiler_params=pltpu.CompilerParams(
             collective_id=0, has_side_effects=True, vmem_limit_bytes=58 * 2**20
         ),
-    )(tokens, gain, wq, wk, wv, wout, cot, gates)
-
-
-def hard_concrete(mask_logit, noise_draw):
-    stretched = jax.nn.sigmoid(
-        (jnp.log(noise_draw) - jnp.log(1.0 - noise_draw) + mask_logit) / BETA
-    )
-    shifted = stretched * (ZETA - GAMMA) + GAMMA
-    gate_value = jnp.clip(shifted, 0.0, 1.0)
-    inside = jnp.logical_and(shifted > 0.0, shifted < 1.0)
-    gate_slope = jnp.where(inside, (ZETA - GAMMA) * stretched * (1.0 - stretched) / BETA, 0.0)
-    expected = jax.nn.sigmoid(mask_logit - BETA * math.log(-GAMMA / ZETA))
-    return (gate_value, gate_slope, PENALTY * expected * (1.0 - expected))
-
-
-def body(tokens, norm_gain, w_query, w_key, value_weight, w_out, mask_logit, noise_draw, cotangent):
-    local_heads = mask_logit.shape[0]
-    inv_root = 1.0 / math.sqrt(tokens.shape[0] * lax.axis_size("ctx"))
-    gate_value, gate_slope, penalty_term = hard_concrete(mask_logit, noise_draw)
-    gate_columns = jnp.repeat(gate_value, HEAD_SIZE)
-    grad_t, out_t, gate_rows = run_layer(
-        tokens, norm_gain.astype(F32)[None, :], w_query, w_key, value_weight, w_out, cotangent, gate_columns[None, :]
-    )
-    layer_out = out_t.T
-    summed = jnp.moveaxis(grad_t, 1, 2).reshape(local_heads * HEAD_SIZE, grad_t.shape[1])
-    grad_out_proj = summed * gate_columns[:, None] * inv_root
-    gate_product = jnp.sum(gate_rows[:local_heads], axis=1)
-    grad_logit = gate_product * inv_root * gate_slope + penalty_term
-    return (layer_out, grad_logit, grad_out_proj)
+    )(tokens, norm_gain, *rest)
+    layer_out, grad_logit, grad_out = pl.pallas_call(
+        deliver_kernel,
+        out_shape=(layer_shape, jax.ShapeDtypeStruct((4,), F32), grad_shape),
+        in_specs=[vmem, smem, vmem],
+        out_specs=(vmem, smem, vmem),
+    )(*results)
+    return layer_out.T, grad_logit, grad_out.T
 
 
 def solution(mesh):

time: 82.2 us -> 73.3 us (0.89)
  other arithmetic: 4.06 us -> 0 us
  local copies, waits for them, and re-layouts: 4.05 us -> 0 us
    mul x1 -> x0, other arithmetic: 2.04 us -> none  [body(): grad_out_proj = summed * gate_columns[:, None] * inv_root]
    unnamed x3 -> x0, local copies, waits for them, and re-layouts: 1.99 us -> none
    broadcast_in_dim x2 -> x0, local copies, waits for them, and re-layouts: 1.99 us -> none  [the longest x1 1.33 us: body(): norm_gain.astype(F32)[None, :]]
    pallas_call x1 -> x2, Pallas kernels: 73.1 us -> 72.3 us  [the longest x1 69.8 us: body(): pl.pallas_call(layer_kernel, out_shape=(layer_shape, jax.ShapeDtypeStruct...]
where the time goes in v3:
time: 73.3 us; the launch traced here: 73.1 us
  Pallas kernels  72.3 us (99%)
  between operations  0.8 us (1%)
    pallas_call x1, Pallas kernels, body(): pl.pallas_call(layer_kernel, out_shape=(layer_shape, jax.ShapeDtypeStruct...  69.8 us
    pallas_call x1, Pallas kernels, body(): pl.pallas_call(deliver_kernel, out_shape=(layer_shape, jax.ShapeDtypeStru...  2.44 us

profile of v3, /device:TPU:0, one launch (start us, length us, event | category | flops | bytes accessed | tf_op | source)
XLA Modules:
  0.0 73.1 jit_solution(2514160314301767227)
XLA Ops:
  0.6 69.8 %shard_map.112 = (bf16[672,512]{1,0:T(8,128)(2,1)}, f32[8,128]{1,0:T(8,128)}, f32[336,512]{1,0:T(8,128)}) custom-call(bf16[512,5376]{1,0:T(8,128)(2,1)} %tokens.1, bf16[5376]{0:T(1024)(128)(2,1)} %gain.1, bf16[5376,512]{1,0:T(8,128)(2,1)} %wq.1, bf16[5376,256]{1,0:T(8,128)(2,1)} %wk.1, bf16[5376,256]{1,0:T(8,128)(2,1)} %wv.1, bf16[512,5376]{1,0:T(8,128)(2,1)} %wout.1, ...), custom_call_target="tpu_custom_call" | custom-call | tf_op jit(solution)/shard_map/pallas_call | solution.py:496
  70.5 2.4 %shard_map.113 = (bf16[672,512]{1,0:T(8,128)(2,1)}, f32[4]{0:T(128)}, f32[336,512]{1,0:T(8,128)}) custom-call(bf16[672,512]{1,0:T(8,128)(2,1)} %get-tuple-element.9.layer_in, f32[8,128]{1,0:T(8,128)} %get-tuple-element.10.gate_in, f32[336,512]{1,0:T(8,128)} %get-tuple-element.11.grad_in), custom_call_target="tpu_custom_call" | custom-call | tf_op jit(solution)/shard_map/pallas_call | solution.py:534

commit v4 on v3

--- a/solution.py
+++ b/solution.py
@@ -175,7 +175,6 @@
     hop0 = pass_on(held(0, 0), held(1, 0), next_block)
     keys_and_values(1)
     back1 = pass_on(held(0, 1), (relay_k, relay_v), at_y(3))
-    hop1 = pass_on(held(0, 1), held(1, 1), next_block)
     weight_loads[4].wait()
     queries[...] = project(second_w[...])
 
@@ -183,6 +182,8 @@
         wout_load(index).start()
 
     def attend(slot, pair):
+        square = (128, 128)
+        triangle = lax.broadcasted_iota(jnp.int32, square, 0) <= lax.broadcasted_iota(jnp.int32, square, 1)
         for block in range(4):
             rows = pl.ds(128 * block, 128)
             start, stop = (0, 128 * (block + 1)) if slot == 0 else (0, 512) if slot == 1 else (128 * block, 512)
@@ -193,10 +194,12 @@
                 scores = lax.dot_general(
                     keys, queries[rows, here], (((1,), (1,)), ((), ())), preferred_element_type=F32
                 )
-                if slot != 1:
-                    key = lax.broadcasted_iota(jnp.int32, scores.shape, 0) + start
-                    query = lax.broadcasted_iota(jnp.int32, scores.shape, 1) + 128 * block
-                    scores = jnp.where(key <= query if slot == 0 else key > query, scores, -jnp.inf)
+                if slot == 0:
+                    last = jnp.where(triangle, scores[128 * block :], -jnp.inf)
+                    scores = jnp.concatenate([scores[: 128 * block], last], axis=0) if block else last
+                elif slot == 2:
+                    edge = jnp.where(triangle, -jnp.inf, scores[:128])
+                    scores = jnp.concatenate([edge, scores[128:]], axis=0) if block < 3 else edge
                 peak = jnp.max(scores, axis=0, keepdims=True)
                 if slot > 0:
                     before = top[one, rows]
@@ -220,16 +223,10 @@
             att[here, :] = result
             gated[here, :] = (wide(result) * gates[number][0:1, 0:1]).astype(BF16)
 
-    gates, slopes, penalties = zip(
-        *(
-            hard_concrete(jnp.full((8, 128), mask_logit[number], F32), jnp.full((8, 128), noise_draw[number], F32))
-            for number in range(4)
-        )
-    )
     attend(0, 0)
-    attend(0, 1)
     arrive(hop0)
     far0 = pass_on(held(1, 0), held(2, 0), next_block)
+    attend(0, 1)
 
     def turn_cot(index, carry):
         cot_load(index).wait()
@@ -238,6 +235,7 @@
         return carry
 
     lax.fori_loop(0, 7, turn_cot, 0)
+    hop1 = pass_on(held(0, 1), held(1, 1), next_block)
     arrive(back1)
     far1 = pass_on((relay_k, relay_v), held(2, 1), two_on)
 
@@ -361,6 +359,12 @@
         out[place] = product.reshape(2, OUT_ROWS, 512)
         across.append(links.start(out.at[place, 1 - core], out_core.at[place], sibling))
 
+    gates, slopes, penalties = zip(
+        *(
+            hard_concrete(jnp.full((8, 128), mask_logit[number], F32), jnp.full((8, 128), noise_draw[number], F32))
+            for number in range(4)
+        )
+    )
     arrive(far0)
 
     @pl.when(ctx >= 2)

time: 73.3 us -> 70.9 us (0.967)
  Pallas kernels: 72.3 us -> 69.9 us
    pallas_call x1, Pallas kernels: 69.8 us -> 67.4 us  [body(): pl.pallas_call(layer_kernel, out_shape=(layer_shape, jax.ShapeDtypeStruct...]
where the time goes in v4:
time: 70.9 us; the launch traced here: 70.7 us
  Pallas kernels  69.9 us (99%)
  between operations  0.8 us (1%)
    pallas_call x1, Pallas kernels, body(): pl.pallas_call(layer_kernel, out_shape=(layer_shape, jax.ShapeDtypeStruct...  67.4 us
    pallas_call x1, Pallas kernels, body(): pl.pallas_call(deliver_kernel, out_shape=(layer_shape, jax.ShapeDtypeStru...  2.44 us

profile of v4, /device:TPU:0, one launch (start us, length us, event | category | flops | bytes accessed | tf_op | source)
XLA Modules:
  0.0 70.7 jit_solution(13766853318946749039)
XLA Ops:
  0.6 67.4 %shard_map.112 = (bf16[672,512]{1,0:T(8,128)(2,1)}, f32[8,128]{1,0:T(8,128)}, f32[336,512]{1,0:T(8,128)}) custom-call(bf16[512,5376]{1,0:T(8,128)(2,1)} %tokens.1, bf16[5376]{0:T(1024)(128)(2,1)} %gain.1, bf16[5376,512]{1,0:T(8,128)(2,1)} %wq.1, bf16[5376,256]{1,0:T(8,128)(2,1)} %wk.1, bf16[5376,256]{1,0:T(8,128)(2,1)} %wv.1, bf16[512,5376]{1,0:T(8,128)(2,1)} %wout.1, ...), custom_call_target="tpu_custom_call" | custom-call | tf_op jit(solution)/shard_map/pallas_call | solution.py:500
  68.1 2.4 %shard_map.113 = (bf16[672,512]{1,0:T(8,128)(2,1)}, f32[4]{0:T(128)}, f32[336,512]{1,0:T(8,128)}) custom-call(bf16[672,512]{1,0:T(8,128)(2,1)} %get-tuple-element.9.layer_in, f32[8,128]{1,0:T(8,128)} %get-tuple-element.10.gate_in, f32[336,512]{1,0:T(8,128)} %get-tuple-element.11.grad_in), custom_call_target="tpu_custom_call" | custom-call | tf_op jit(solution)/shard_map/pallas_call | solution.py:538

commit v5 on v4

--- a/solution.py
+++ b/solution.py
@@ -405,13 +405,13 @@
 
     far, after, before = order[0], order[1], order[2]
     upper, lower = pl.ds(0, HALF_OUT), pl.ds(HALF_OUT, HALF_OUT)
+    relay_first(0)
+    relay_first(1)
     add_core(0)
     ring = [
         links.start(out_core.at[far, upper], out_in.at[0], at_z(1)),
         links.start(out_core.at[far, lower], out_in.at[1], at_z(3)),
     ]
-    relay_first(0)
-    relay_first(1)
     grad_pair(1)
     send_first(2)
     send_first(3)

time: 70.9 us -> 70.6 us (level); the launches traced: 70.7 us -> 69.5 us
  Pallas kernels: 69.9 us -> 68.7 us
    pallas_call x1, Pallas kernels: 67.4 us -> 66.2 us  [body(): pl.pallas_call(layer_kernel, out_shape=(layer_shape, jax.ShapeDtypeStruct...]
where the time goes in v5:
time: 70.6 us; the launch traced here: 69.5 us
  Pallas kernels  68.7 us (97%)
  between operations  0.8 us (1%)
    pallas_call x1, Pallas kernels, body(): pl.pallas_call(layer_kernel, out_shape=(layer_shape, jax.ShapeDtypeStruct...  66.2 us
    pallas_call x1, Pallas kernels, body(): pl.pallas_call(deliver_kernel, out_shape=(layer_shape, jax.ShapeDtypeStru...  2.44 us

profile of v5, /device:TPU:0, one launch (start us, length us, event | category | flops | bytes accessed | tf_op | source)
XLA Modules:
  0.0 69.5 jit_solution(5828556419038005401)
XLA Ops:
  0.6 66.2 %shard_map.112 = (bf16[672,512]{1,0:T(8,128)(2,1)}, f32[8,128]{1,0:T(8,128)}, f32[336,512]{1,0:T(8,128)}) custom-call(bf16[512,5376]{1,0:T(8,128)(2,1)} %tokens.1, bf16[5376]{0:T(1024)(128)(2,1)} %gain.1, bf16[5376,512]{1,0:T(8,128)(2,1)} %wq.1, bf16[5376,256]{1,0:T(8,128)(2,1)} %wk.1, bf16[5376,256]{1,0:T(8,128)(2,1)} %wv.1, bf16[512,5376]{1,0:T(8,128)(2,1)} %wout.1, ...), custom_call_target="tpu_custom_call" | custom-call | tf_op jit(solution)/shard_map/pallas_call | solution.py:500
  66.8 2.4 %shard_map.113 = (bf16[672,512]{1,0:T(8,128)(2,1)}, f32[4]{0:T(128)}, f32[336,512]{1,0:T(8,128)}) custom-call(bf16[672,512]{1,0:T(8,128)(2,1)} %get-tuple-element.9.layer_in, f32[8,128]{1,0:T(8,128)} %get-tuple-element.10.gate_in, f32[336,512]{1,0:T(8,128)} %get-tuple-element.11.grad_in), custom_call_target="tpu_custom_call" | custom-call | tf_op jit(solution)/shard_map/pallas_call | solution.py:538
